TPU v7x, 128 devices: a whole 4x4x4 slice. The times are simulated.
128 devices in a mesh: px: 8 (over z_hi, x), py: 16 (over z_lo, y, core).
Axes of the slice: x: 4, y: 4, z: 4 (z_hi: 2, z_lo: 2; z = z_hi * 2 + z_lo), core: 2. Of those that a mesh axis runs over, the one named last changes fastest.
Arguments:
- rho_hat: float32 [2, 128, 768, 768], P(None, 'px', 'py'), may hold values from -6 to 6
Outputs:
- v_hat: float32 [2, 128, 768, 768], P(None, 'px', 'py')
All inputs are finite; a program needn't handle non-finite values.
Results may differ from a plain program's by a relative error of at most 0.0003.
Values sent between devices are 32-bit elements; how exact they have to be, the bound alone decides.
No kernel may reach another device: no remote copies, remote signals or barrier semaphores. Data moves between devices by JAX's collectives and lax.ppermute only.
A program may use at most 192 MiB of HBM per device.

v0:
```python
import math

import jax
import jax.numpy as jnp
from jax import lax
from jax.sharding import PartitionSpec as P

grid_step = 0.25
density_floor = 0.02
density_scale = 0.2
kappa_value = 0.804
mu_value = 0.2195149727645171
beta_value = 0.06672455060314922
gamma_value = (1.0 - math.log(2.0)) / (math.pi * math.pi)
correlation_scale = 0.031091
correlation_alpha = 0.2137
correlation_terms = (7.5957, 3.5876, 1.6382, 0.49294)


def with_halo(cells, sides, width):
    for axis, dim in sides:
        count = lax.axis_size(axis)
        head = lax.slice_in_dim(cells, 0, width, axis=dim)
        tail = lax.slice_in_dim(cells, cells.shape[dim] - width, cells.shape[dim], axis=dim)
        cells = jnp.concatenate(
            [
                lax.ppermute(tail, axis, [(i, (i + 1) % count) for i in range(count)]),
                cells,
                lax.ppermute(head, axis, [((i + 1) % count, i) for i in range(count)]),
            ],
            axis=dim,
        )
    return cells


def energy_density(rho, sigma):
    cube = jnp.cbrt(rho)
    k_fermi = (3.0 * math.pi * math.pi) ** (1.0 / 3.0) * cube
    exchange_unif = -0.75 * (3.0 / math.pi) ** (1.0 / 3.0) * cube * rho
    s_square = sigma / (4.0 * k_fermi * k_fermi * rho * rho)
    enhance = 1.0 + kappa_value - kappa_value / (1.0 + mu_value * s_square / kappa_value)
    radius = (3.0 / (4.0 * math.pi)) ** (1.0 / 3.0) / cube
    root = jnp.sqrt(radius)
    denom = (
        2.0
        * correlation_scale
        * (
            correlation_terms[0] * root
            + correlation_terms[1] * radius
            + correlation_terms[2] * radius * root
            + correlation_terms[3] * radius * radius
        )
    )
    uniform_corr = (
        -2.0 * correlation_scale * (1.0 + correlation_alpha * radius) * jnp.log(1.0 + 1.0 / denom)
    )
    screen_square = 4.0 * k_fermi / math.pi
    t_square = sigma / (4.0 * screen_square * rho * rho)
    coefficient = beta_value / gamma_value / (jnp.exp(-uniform_corr / gamma_value) - 1.0)
    scaled = coefficient * t_square
    gradient_term = gamma_value * jnp.log(
        1.0
        + beta_value / gamma_value * t_square * (1.0 + scaled) / (1.0 + scaled + scaled * scaled)
    )
    return exchange_unif * enhance + rho * (uniform_corr + gradient_term)


def phase_table(count_rows, count_cols, length):
    row_index = jnp.arange(count_rows, dtype=jnp.int32)
    col_index = jnp.arange(count_cols, dtype=jnp.int32)
    angle = (row_index[:, None] * col_index[None, :] % length).astype(jnp.float32) * (
        2.0 * math.pi / length
    )
    return (jnp.cos(angle), jnp.sin(angle))


def clamp_depth(field):
    return jnp.concatenate([field[:1], field, field[-1:]], axis=0)


def smooth_depth(field):
    padded = clamp_depth(field)
    return 0.25 * padded[:-2] + 0.5 * padded[1:-1] + 0.25 * padded[2:]


def slope_depth(field):
    padded = clamp_depth(field)
    return (padded[2:] - padded[:-2]) / (2.0 * grid_step)


def smooth_plane(field):
    field = 0.25 * field[:, :, :-2] + 0.5 * field[:, :, 1:-1] + 0.25 * field[:, :, 2:]
    field = 0.25 * field[:, :-2] + 0.5 * field[:, 1:-1] + 0.25 * field[:, 2:]
    return smooth_depth(field)


def gradients(smooth):
    center = smooth[:, 1:-1, 1:-1]
    grad_x = (smooth[:, 1:-1, 2:] - smooth[:, 1:-1, :-2]) / (2.0 * grid_step)
    grad_y = (smooth[:, 2:, 1:-1] - smooth[:, :-2, 1:-1]) / (2.0 * grid_step)
    grad_z = slope_depth(center)
    return (center, grad_x, grad_y, grad_z)


def local_terms(center, grad_x, grad_y, grad_z):
    sigma = grad_x * grad_x + grad_y * grad_y + grad_z * grad_z
    energy, pullback = jax.vjp(energy_density, center, sigma)
    d_rho, d_sigma = pullback(jnp.ones_like(energy))
    return (d_rho, 2.0 * d_sigma * grad_x, 2.0 * d_sigma * grad_y, 2.0 * d_sigma * grad_z)


def divergence(flux_x, flux_y, inner_z):
    along_x = (flux_x[:, 1:-1, 2:] - flux_x[:, 1:-1, :-2]) / (2.0 * grid_step)
    along_y = (flux_y[:, 2:, 1:-1] - flux_y[:, :-2, 1:-1]) / (2.0 * grid_step)
    return along_x + along_y + slope_depth(inner_z)


def on_device(rho_hat):
    highest = lax.Precision.HIGHEST
    width_y = rho_hat.shape[3]
    width_x = rho_hat.shape[2] * lax.axis_size("py")
    norm_y = 1.0 / math.sqrt(width_y)
    norm_x = 1.0 / math.sqrt(width_x)
    cosine_rows, sine_rows = phase_table(width_y, width_y, width_y)
    cosine_columns, sine_columns = phase_table(width_x, width_x, width_x)
    inverse_rows = (
        jnp.stack(
            [jnp.stack([cosine_rows, sine_rows], 1), jnp.stack([-sine_rows, cosine_rows], 1)], 0
        )
        * norm_y
    )
    inverse_columns = jnp.stack([cosine_columns, -sine_columns], 0) * norm_x
    forward_columns = jnp.stack([cosine_columns, -sine_columns], 1) * norm_x
    columns = jnp.einsum("czxk,ckdy->dzyx", rho_hat, inverse_rows, precision=highest)
    real_part = jnp.einsum(
        "czyk,ckx->zyx",
        lax.all_to_all(columns, "py", split_axis=2, concat_axis=3, tiled=True),
        inverse_columns,
        precision=highest,
    )
    rows = density_floor + density_scale * jax.nn.softplus(real_part)
    brick = lax.all_to_all(rows, "px", split_axis=2, concat_axis=0, tiled=True)
    padded = with_halo(brick, (("px", 2), ("py", 1)), 2)
    center, grad_x, grad_y, grad_z = gradients(smooth_plane(padded))
    inner_rho, flux_x, flux_y, inner_z = local_terms(center, grad_x, grad_y, grad_z)
    sides = with_halo(jnp.stack([flux_x, flux_y]), (("px", 3), ("py", 2)), 1)
    flux_x = sides[0]
    flux_y = sides[1]
    potential = inner_rho - divergence(flux_x, flux_y, inner_z)
    spectral_rows = jnp.einsum(
        "zyx,xck->zcky",
        lax.all_to_all(potential, "px", split_axis=0, concat_axis=2, tiled=True),
        forward_columns,
        precision=highest,
    )
    forward_rows = (
        jnp.stack(
            [jnp.stack([cosine_rows, -sine_rows], 1), jnp.stack([sine_rows, cosine_rows], 1)], 0
        )
        * norm_y
    )
    spectra = jnp.einsum(
        "zcxy,cydk->dzxk",
        lax.all_to_all(spectral_rows, "py", split_axis=2, concat_axis=3, tiled=True),
        forward_rows,
        precision=highest,
    )
    local_waves = spectra.shape[2]
    wave_x = lax.axis_index("py") * local_waves + jnp.arange(local_waves, dtype=jnp.int32)
    wave_y = jnp.arange(spectra.shape[3], dtype=jnp.int32)
    anchor = (wave_x[:, None] == 0) & (wave_y[None, :] == 0)
    return jnp.where(anchor[None, None], jnp.float32(0.0), spectra)


def solution(mesh):
    return jax.shard_map(
        on_device,
        mesh=mesh,
        in_specs=(P(None, "px", "py", None),),
        out_specs=P(None, "px", "py", None),
        check_vma=False,
    )
```

profile of v0, /device:TPU:14, one launch (start us, length us, event | category | flops | bytes accessed | tf_op | source)
XLA Modules:
  0.0 642.8 jit_solution(3778381564046463243)
XLA Ops:
  0.0 9.5 %fusion.79 = (f32[768,1,768]{2,0,1:T(8,128)S(1)}, f32[768,1,768]{2,0,1:T(8,128)S(1)}) fusion(), kind=kLoop, calls=%fused_computation.136 | loop fusion | flops 5308416 | bytes 4718592 | tf_op jit(solution)/shard_map/sin | solution.py:74
  22.9 25.9 %fusion.86 = f32[2,16,768,48]{2,3,1,0:T(8,128)} fusion(f32[2,16,48,768]{3,2,1,0:T(8,128)S(1)} %bitcast.132, f32[1,768,2,768]{3,1,2,0:T(8,128)S(1)} %get-tuple-element.13, f32[1,768,2,768]{3,1,2,0:T(8,128)S(1)} %get-tuple-element.26), kind=kOutput, calls=%fused_computation.141 | convolution fusion | flops 21747990528 | bytes 18874368 | tf_op jit(solution)/shard_map/czxk,ckdy->dzyx/dot_general | solution.py:134
  48.9 12.0 %copy.55 = f32[2,16,768,48]{3,1,0,2:T(8,128)} copy(f32[2,16,768,48]{2,3,1,0:T(8,128)} %fusion.86) | data formatting | bytes 9437184 | tf_op jit(solution)/shard_map/czxk,ckdy->dzyx/transpose | solution.py:134
  60.9 17.7 %reshape.166 = f32[16,1,73728]{2,1,0:T(1,128)} reshape(f32[768,2,16,48]{3,2,1,0:T(8,128)} %bitcast.118) | data formatting | bytes 9437184
  84.8 10.5 %sine_negate_fusion = (f32[1,768,768]{2,1,0:T(8,128)S(1)}, f32[1,768,768]{2,1,0:T(8,128)}) fusion(), kind=kLoop, calls=%fused_computation.127 | loop fusion | flops 5898240 | bytes 4718592 | tf_op jit(solution)/shard_map/neg | solution.py:158
  95.3 53.6 %all-to-all-done = f32[16,1,73728]{2,1,0:T(1,128)} async-done(((f32[16,1,73728]{2,1,0:T(1,128)}), f32[16,1,73728]{2,1,0:T(1,128)}, u32[]{:S(2)}, u32[]{:S(2)}) %all-to-all-start) | async-done | bytes 4718624 | tf_op jit(solution)/shard_map/all_to_all | solution.py:137
  149.5 15.9 %reduce = f32[16,73728]{1,0:T(8,128)} reduce(f32[16,1,73728]{2,1,0:T(1,128)} %all-to-all-done, f32[]{:T(128)} %broadcast.469), dimensions={1}, to_apply=%all_to_all.52.reduce_sub_computation | reduce | bytes 9437188 | tf_op jit(solution)/shard_map/all_to_all | solution.py:137
  165.4 13.8 %reshape.167 = f32[768,2,16,48]{3,2,1,0:T(8,128)} reshape(f32[16,73728]{1,0:T(8,128)} %reduce) | data formatting | bytes 9437184
  179.2 16.4 %copy.93 = f32[2,16,16,48,48]{4,2,3,0,1:T(8,128)} copy(f32[2,16,16,48,48]{4,1,0,3,2:T(8,128)} %bitcast.114) | data formatting | bytes 9437184 | tf_op jit(solution)/shard_map/all_to_all | solution.py:137
  195.6 10.9 %all_to_all.55 = f32[2,16,48,768]{3,2,0,1:T(8,128)} reshape(f32[2,16,48,16,48]{4,3,2,0,1:T(8,128)} %bitcast.115) | data formatting | bytes 9437184 | tf_op jit(solution)/shard_map/all_to_all | solution.py:137
  206.5 16.7 %fusion.52 = f32[16,48,768]{2,1,0:T(8,128)} fusion(f32[2,16,48,768]{3,2,0,1:T(8,128)} %all_to_all.55, f32[1,768,768]{2,1,0:T(8,128)S(1)} %get-tuple-element.34, f32[1,768,768]{2,1,0:T(8,128)} %get-tuple-element.35), kind=kOutput, calls=%fused_computation.79 | convolution fusion | flops 10878713856 | bytes 11796480 | tf_op jit(solution)/shard_map/czyk,ckx->zyx/dot_general | solution.py:135
  239.1 37.7 %all_to_all.72 = f32[8,1,73728]{2,1,0:T(1,128)S(1)} all-to-all(f32[8,1,73728]{2,1,0:T(1,128)} %reshape.168), channel_id=1, replica_groups=mesh['px'=8,'py'=16] {'px'}, dimensions={0} | all-to-all | bytes 4718592 | tf_op jit(solution)/shard_map/all_to_all | solution.py:142
  328.0 12.1 %multiply_bitcast_fusion.1 = (f32[1,128,48,96]{1,3,2,0:T(8,128)S(1)}, f32[128,48,96]{0,2,1:T(8,128)}, f32[128,48,96]{0,2,1:T(8,128)}) fusion(f32[128,50,98]{0,2,1:T(8,128)S(1)} %fusion.26, f32[128,48,96]{0,2,1:T(8,128)S(1)} %slice.166, f32[1,48,96]{0,2,1:T(8,128)S(1)} %get-tuple-element.21, f32[1,48,96]{0,2,1:T(8,128)S(1)} %get-tuple-element.20), kind=kLoop, calls=%fused_computation.103 | loop fusion | flops 50724864 | bytes 21270528 | tf_op jit(solution)/shard_map/stack | solution.py:146
  360.9 19.5 %fusion.45 = f32[128,48,96]{0,2,1:T(8,128)} fusion(f32[128,48,96]{0,2,1:T(8,128)S(1)} %get-tuple-element.29, f32[1,48,96]{0,2,1:T(8,128)S(1)} %get-tuple-element.31, f32[1,48,96]{0,2,1:T(8,128)S(1)} %get-tuple-element.30, f32[128,50,98]{0,2,1:T(8,128)S(1)} %get-tuple-element.9, f32[128,50,98]{0,2,1:T(8,128)S(1)} %get-tuple-element.8, ...), kind=kLoop, calls=%fused_computation.72 | loop fusion | flops 93782016 | bytes 18911232 | tf_op jit(solution)/shard_map/sub | solution.py:149
  382.9 44.5 %all_to_all.73 = f32[128,48,96]{2,1,0:T(8,128)S(1)} all-to-all(f32[128,48,96]{2,1,0:T(8,128)S(1)} %copy.68), channel_id=1, replica_groups=mesh['px'=8,'py'=16] {'px'}, dimensions={0} | all-to-all | bytes 4718592 | tf_op jit(solution)/shard_map/all_to_all | solution.py:152
  435.4 15.3 %fusion.83 = f32[16,2,768,48]{2,3,0,1:T(8,128)} fusion(f32[16,48,768,1]{2,1,0,3:T(8,128)} %reshape.160, f32[768,1,768]{2,0,1:T(8,128)} %copy-done.4, f32[768,1,768]{2,0,1:T(8,128)S(1)} %copy-done.3), kind=kOutput, calls=%fused_computation.140 | convolution fusion | flops 10873995264 | bytes 11796480 | tf_op jit(solution)/shard_map/zyx,xck->zcky/dot_general | solution.py:150
  450.8 12.0 %copy.70 = f32[16,2,768,48]{3,0,1,2:T(8,128)} copy(f32[16,2,768,48]{2,3,0,1:T(8,128)} %fusion.83) | data formatting | bytes 9437184 | tf_op jit(solution)/shard_map/zyx,xck->zcky/transpose | solution.py:150
  462.8 17.7 %reshape.170 = f32[16,1,73728]{2,1,0:T(1,128)} reshape(f32[768,2,16,48]{3,2,1,0:T(8,128)} %bitcast.119) | data formatting | bytes 9437184
  487.7 63.7 %all-to-all-done.3 = f32[16,1,73728]{2,1,0:T(1,128)} async-done(((f32[16,1,73728]{2,1,0:T(1,128)}), f32[16,1,73728]{2,1,0:T(1,128)}, u32[]{:S(2)}, u32[]{:S(2)}) %all-to-all-start.3) | async-done | bytes 4718624 | tf_op jit(solution)/shard_map/all_to_all | solution.py:164
  551.4 15.9 %reduce.2 = f32[16,73728]{1,0:T(8,128)} reduce(f32[16,1,73728]{2,1,0:T(1,128)} %all-to-all-done.3, f32[]{:T(128)} %broadcast.469), dimensions={1}, to_apply=%all_to_all.64.reduce_sub_computation | reduce | bytes 9437188 | tf_op jit(solution)/shard_map/all_to_all | solution.py:164
  567.3 13.6 %reshape.171 = f32[768,2,16,48]{3,2,1,0:T(8,128)} reshape(f32[16,73728]{1,0:T(8,128)} %reduce.2) | data formatting | bytes 9437184
  580.9 16.4 %copy.92 = f32[16,2,16,48,48]{4,2,3,1,0:T(8,128)} copy(f32[16,2,16,48,48]{4,0,1,3,2:T(8,128)} %bitcast.116) | data formatting | bytes 9437184 | tf_op jit(solution)/shard_map/all_to_all | solution.py:164
  597.3 11.1 %reshape.162 = f32[16,2,48,768,1]{3,2,1,0,4:T(8,128)} reshape(f32[16,2,48,16,48]{4,3,2,1,0:T(8,128)} %bitcast.117) | data formatting | bytes 9437184 | tf_op jit(solution)/shard_map/all_to_all | solution.py:164
  608.4 34.2 %bitcast_select_fusion = f32[2,16,48,768]{3,2,1,0:T(8,128)} fusion(pred[48,768]{1,0:T(8,128)(4,1)S(1)} %broadcast_and_fusion, f32[16,2,48,768,1]{3,2,1,0,4:T(8,128)} %reshape.162, f32[1,768,2,768]{3,1,0,2:T(8,128)} %get-tuple-element.27, f32[1,768,2,768]{3,1,0,2:T(8,128)} %get-tuple-element.12), kind=kOutput, calls=%fused_computation.25 | convolution fusion | flops 21749170176 | bytes 18911232 | tf_op jit(solution)/shard_map/zcxy,cydk->dzxk/dot_general | solution.py:162
  (71 shorter events, 125.8 us)
Async XLA Ops:
  9.5 13.4 %copy-start.2 = (f32[768,1,768]{2,0,1:T(8,128)}, f32[768,1,768]{2,0,1:T(8,128)S(1)}, u32[]{:S(2)}) copy-start(f32[768,1,768]{2,0,1:T(8,128)S(1)} %get-tuple-element.33) | copy-start | bytes 7077892
  9.5 13.4 %slice-start = ((s8[4718592]{0:T(1024)(128)(4,1)}), s8[4194304]{0:T(1024)(128)(4,1)S(1)}, s32[]{:S(2)}) async-start(s8[4718592]{0:T(1024)(128)(4,1)} %bitcast.131), calls=%async_computation.4 | async-start | bytes 8388608
  18.6 4.3 copy-start.4
  18.6 4.3 slice-start.1
  78.5 70.4 %all-to-all-start = ((f32[16,1,73728]{2,1,0:T(1,128)}), f32[16,1,73728]{2,1,0:T(1,128)}, u32[]{:S(2)}, u32[]{:S(2)}) async-start(f32[16,1,73728]{2,1,0:T(1,128)} %reshape.166), calls=%async_computation | async-start | bytes 9437184 | tf_op jit(solution)/shard_map/all_to_all | solution.py:137
  303.0 6.9 %collective-permute-start = (f32[128,48,2]{0,1,2:T(8,128)S(1)}, f32[128,48,2]{0,1,2:T(8,128)S(1)}, u32[]{:S(2)}, u32[]{:S(2)}) collective-permute-start(f32[128,48,2]{0,1,2:T(8,128)S(1)} %copy.59), channel_id=1, source_target_pairs={{0,16},{16,32},{32,48},{48,64},{64,80},{80,96},{96,112},{112,0},{1... | collective-permute-start | bytes 147464 | tf_op jit(solution)/shard_map/ppermute | solution.py:27
  307.3 7.9 %collective-permute-start.1 = (f32[128,48,2]{0,1,2:T(8,128)S(1)}, f32[128,48,2]{0,1,2:T(8,128)S(1)}, u32[]{:S(2)}, u32[]{:S(2)}) collective-permute-start(f32[128,48,2]{0,1,2:T(8,128)S(1)} %copy.60), channel_id=1, source_target_pairs={{16,0},{32,16},{48,32},{64,48},{80,64},{96,80},{112,96},{0,112},{1... | collective-permute-start | bytes 147464 | tf_op jit(solution)/shard_map/ppermute | solution.py:29
  309.9 10.6 %copy-start.5 = (f32[128,48,96]{0,2,1:T(8,128)S(1)}, f32[128,48,96]{0,2,1:T(8,128)}, u32[]{:S(2)}) copy-start(f32[128,48,96]{0,2,1:T(8,128)} %copy.62) | copy-start | bytes 7077892
  316.2 4.2 collective-permute-start.2
  316.3 4.1 collective-permute-start.3
  325.8 1.4 copy-start
  325.8 2.1 copy-start.1
  345.1 4.2 collective-permute-start.4
  345.5 7.7 %collective-permute-start.5 = (f32[2,128,48,1]{1,2,3,0:T(8,128)S(1)}, f32[2,128,48,1]{1,2,3,0:T(8,128)S(1)}, u32[]{:S(2)}, u32[]{:S(2)}) collective-permute-start(f32[2,128,48,1]{1,2,3,0:T(8,128)S(1)} %bitcast.129), channel_id=1, source_target_pairs={{16,0},{32,16},{48,32},{64,48},{80,64},{96,80},{112,96},{0,112},{1... | collective-permute-start | bytes 147464 | tf_op jit(solution)/shard_map/ppermute | solution.py:29
  353.2 4.6 collective-permute-start.6
  353.7 4.1 collective-permute-start.7
  359.3 1.7 copy-start.6
  430.9 4.6 copy-start.3
  480.4 71.0 %all-to-all-start.3 = ((f32[16,1,73728]{2,1,0:T(1,128)}), f32[16,1,73728]{2,1,0:T(1,128)}, u32[]{:S(2)}, u32[]{:S(2)}) async-start(f32[16,1,73728]{2,1,0:T(1,128)} %reshape.170), calls=%async_computation.3 | async-start | bytes 9437184 | tf_op jit(solution)/shard_map/all_to_all | solution.py:164
where the time goes:
time: 655 us; the launch traced here: 643 us
  local copies, waits for them, and re-layouts  197 us (30%)
  waiting for transfers between devices  133 us (20%)
  other arithmetic  116 us (18%)
  matrix products  92.1 us (14%)
  blocking collectives  82.2 us (13%)
  starting transfers between devices  21.8 us (3%)
    unnamed x24, local copies, waits for them, and re-layouts  82.3 us
    all_to_all x1, waiting for transfers between devices, on_device(): lax.all_to_all(spectral_rows, 'py', split_axis=2, concat_axis=3, tiled=True)  63.7 us
    all_to_all x1, waiting for transfers between devices, on_device(): lax.all_to_all(columns, 'py', split_axis=2, concat_axis=3, tiled=True)  53.6 us
    all_to_all x1, blocking collectives, on_device(): lax.all_to_all(potential, 'px', split_axis=0, concat_axis=2, tiled=True)  44.5 us
    all_to_all x1, blocking collectives, on_device(): brick = lax.all_to_all(rows, 'px', split_axis=2, concat_axis=0, tiled=True)  37.7 us
    dot_general x1, matrix products, on_device(): jnp.einsum('zcxy,cydk->dzxk', lax.all_to_all(spectral_rows, 'py', split_a...  34.2 us
    all_to_all x3, local copies, waits for them, and re-layouts, on_device(): lax.all_to_all(columns, 'py', split_axis=2, concat_axis=3, tiled=True)  27.9 us
    all_to_all x2, local copies, waits for them, and re-layouts, on_device(): lax.all_to_all(spectral_rows, 'py', split_axis=2, concat_axis=3, tiled=True)  27.5 us
  transfers between devices with their start and end apart: 10, of which 7 were waited for; matrix products, arithmetic and copies ran while one was open for 3% of the time, Pallas kernels for 0%

commit v1 on v0

v1 whole, which is shorter than its diff:
```python
import math

import jax
import jax.numpy as jnp
import numpy as np
from jax import lax
from jax.experimental import pallas as pl
from jax.experimental.pallas import tpu as pltpu
from jax.sharding import PartitionSpec as P

grid_step = 0.25
density_floor = 0.02
density_scale = 0.2
kappa_value = 0.804
mu_value = 0.2195149727645171
beta_value = 0.06672455060314922
gamma_value = (1.0 - math.log(2.0)) / (math.pi * math.pi)
correlation_scale = 0.031091
correlation_alpha = 0.2137
correlation_terms = (7.5957, 3.5876, 1.6382, 0.49294)

f32 = jnp.float32
bf16 = jnp.bfloat16
reach = 3
lead = 9


def params(mib):
    return pltpu.CompilerParams(vmem_limit_bytes=mib << 20)


def call(body, out, mib, **options):
    return pl.pallas_call(body, out_shape=out, compiler_params=params(mib), **options)


def split(value):
    high = value.astype(bf16)
    return high, (value - high.astype(f32)).astype(bf16)


def dot_nt(left, right):
    return lax.dot_general(left, right, (((1,), (1,)), ((), ())), preferred_element_type=f32)


def dot_nn(left, right):
    return lax.dot_general(left, right, (((1,), (0,)), ((), ())), preferred_element_type=f32)


def triple(dot, left_high, left_low, right_high, right_low):
    return dot(left_high, right_high) + (dot(left_low, right_high) + dot(left_high, right_low))


def tables_body(stride, coarse_ref, fine_ref, ch_ref, cl_ref, sh_ref, sl_ref):
    fine_cos, fine_sin = fine_ref[0], fine_ref[1]
    for a in range(coarse_ref.shape[1]):
        cos_a, sin_a = coarse_ref[0, a : a + 1], coarse_ref[1, a : a + 1]
        rows = slice(stride * a, stride * (a + 1))
        ch_ref[rows], cl_ref[rows] = split(cos_a * fine_cos - sin_a * fine_sin)
        sh_ref[rows], sl_ref[rows] = split(sin_a * fine_cos + cos_a * fine_sin)


def phase_tables(length, stride):
    def waves(rows, scale):
        angle = (np.outer(rows, np.arange(length)) % length) * (2.0 * math.pi / length)
        return np.stack([np.cos(angle), np.sin(angle)]).astype(np.float32) * np.float32(scale)

    coarse = waves(np.arange(0, length, stride), 1.0)
    fine = waves(np.arange(stride), 1.0 / math.sqrt(length))
    out = [jax.ShapeDtypeStruct((length, length), bf16)] * 4
    body = lambda *refs: tables_body(stride, *refs)
    return call(body, out, 32, name="tables")(jnp.asarray(coarse), jnp.asarray(fine))


def inverse_rows_body(x_ref, ch_ref, cl_ref, sh_ref, sl_ref, out_ref, high_ref, low_ref):
    rows = high_ref.shape[1]
    width = x_ref.shape[3]
    for c in range(2):
        high_ref[c], low_ref[c] = split(x_ref[c].reshape(rows, width))
    group = 4
    block = out_ref.shape[2]

    def step(m, carry):
        at = pl.ds(pl.multiple_of(m * group * block, group * block), group * block)
        ch, cl, sh, sl = ch_ref[at], cl_ref[at], sh_ref[at], sl_ref[at]
        real = (high_ref[0], low_ref[0])
        imag = (high_ref[1], low_ref[1])
        out_re = triple(dot_nt, ch, cl, *real) - triple(dot_nt, sh, sl, *imag)
        out_im = triple(dot_nt, sh, sl, *real) + triple(dot_nt, ch, cl, *imag)
        to = pl.ds(m * group, group)
        out_ref[to, 0] = out_re.reshape(group, block, rows)
        out_ref[to, 1] = out_im.reshape(group, block, rows)
        return carry

    lax.fori_loop(0, out_ref.shape[0] // group, step, 0)


def whole(shape):
    return pl.BlockSpec(shape, lambda *_: (0,) * len(shape))


def inverse_rows(rho_hat, tables, parts, steps):
    _, depth, local, width = rho_hat.shape
    planes = depth // steps
    block = width // parts
    rows = planes * local
    return call(
        inverse_rows_body,
        jax.ShapeDtypeStruct((parts, 2, block, depth * local), f32),
        48,
        grid=(steps,),
        in_specs=[pl.BlockSpec((2, planes, local, width), lambda i: (0, i, 0, 0))]
        + [whole((width, width))] * 4,
        out_specs=pl.BlockSpec((parts, 2, block, rows), lambda i: (0, 0, 0, i)),
        scratch_shapes=[pltpu.VMEM((2, rows, width), bf16), pltpu.VMEM((2, rows, width), bf16)],
        name="inverse_rows",
    )(rho_hat, *tables)


def gather_blocks(in_ref, high_ref, low_ref):
    parts, _, rows, lanes = in_ref.shape
    local = high_ref.shape[2] // parts
    for z in range(lanes // local):
        at = slice(z * local, (z + 1) * local)
        to = slice(z * rows, (z + 1) * rows)
        for c in range(2):
            joined = jnp.concatenate([in_ref[s, c, :, at] for s in range(parts)], axis=-1)
            high_ref[c, to], low_ref[c, to] = split(joined)


def inverse_columns_body(in_ref, ch_ref, cl_ref, sh_ref, sl_ref, out_ref, high_ref, low_ref):
    gather_blocks(in_ref, high_ref, low_ref)
    planes, rows, width = out_ref.shape
    group = planes // 2

    def step(m, carry):
        at = pl.ds(pl.multiple_of(m * group * rows, group * rows), group * rows)
        field = triple(dot_nn, high_ref[0, at], low_ref[0, at], ch_ref[...], cl_ref[...])
        field = field - triple(dot_nn, high_ref[1, at], low_ref[1, at], sh_ref[...], sl_ref[...])
        soft = jnp.maximum(field, 0.0) + jnp.log1p(jnp.exp(-jnp.abs(field)))
        density = density_floor + density_scale * soft
        out_ref[pl.ds(m * group, group)] = density.reshape(group, rows, width)
        return carry

    lax.fori_loop(0, 2, step, 0)


def inverse_columns(blocks, tables, steps):
    parts, _, rows, lanes = blocks.shape
    width = tables[0].shape[0]
    depth = lanes * parts // width
    planes = depth // steps
    scratch = pltpu.VMEM((2, planes * rows, width), bf16)
    return call(
        inverse_columns_body,
        jax.ShapeDtypeStruct((depth, rows, width), f32),
        48,
        grid=(steps,),
        in_specs=[pl.BlockSpec((parts, 2, rows, lanes // steps), lambda i: (0, 0, 0, i))]
        + [whole((width, width))] * 4,
        out_specs=pl.BlockSpec((planes, rows, width), lambda i: (i, 0, 0)),
        scratch_shapes=[scratch, scratch],
        name="inverse_columns",
    )(blocks, *tables)


def shift(value, axis, up):
    count = lax.axis_size(axis)
    pairs = [(i, (i + 1) % count) for i in range(count)]
    return lax.ppermute(value, axis, pairs if up else [(b, a) for a, b in pairs])


def edges_body(low_ref, first_ref, last_ref, high_ref, head_ref, tail_ref):
    depth = first_ref.shape[0]
    rows = low_ref.shape[1]
    for z in range(depth + 2 * reach):
        to = slice(reach * z, reach * (z + 1))
        if z < reach:
            head, tail = low_ref[z, :reach], low_ref[z, rows - reach :]
        elif z < depth + reach:
            head, tail = first_ref[z - reach, :reach], last_ref[z - reach, 8 - reach :]
        else:
            y = z - depth - reach
            head, tail = high_ref[y, :reach], high_ref[y, rows - reach :]
        head_ref[to], tail_ref[to] = head, tail


def edges(below, density, above):
    depth, rows, width = density.shape
    count = -(-(depth + 2 * reach) * reach // 8) * 8
    slab = whole((reach, rows, width))
    side = lambda at: pl.BlockSpec((depth, 8, width), lambda i: (0, at, 0))
    return call(
        edges_body,
        [jax.ShapeDtypeStruct((count, width), f32)] * 2,
        16,
        grid=(1,),
        in_specs=[slab, side(0), side(rows // 8 - 1), slab],
        out_specs=[whole((count, width))] * 2,
        name="edges",
    )(below, density, density, above)


def roll_x(value, by):
    return pltpu.roll(value, by % value.shape[-1], value.ndim - 1)


def energy_slopes(rho, sigma):
    two_a = 2.0 * correlation_scale
    b1, b2, b3, b4 = correlation_terms
    sixth = jnp.exp(jnp.log(rho) * (-1.0 / 6.0))
    inv = sixth * sixth
    inv2 = inv * inv
    inv4 = inv2 * inv2
    cube = rho * inv2
    exchange = -0.75 * (3.0 / math.pi) ** (1.0 / 3.0)
    s_scale = 0.25 / (3.0 * math.pi**2) ** (2.0 / 3.0)
    scaled_sigma = sigma * inv4
    s_square = s_scale * scaled_sigma * inv4
    weight = 1.0 / (1.0 + (mu_value / kappa_value) * s_square)
    enhance = (1.0 + kappa_value) - kappa_value * weight
    steep = mu_value * weight * weight
    x_rho = (exchange * cube) * ((4.0 / 3.0) * enhance - (8.0 / 3.0) * steep * s_square)
    radius_scale = (3.0 / (4.0 * math.pi)) ** (1.0 / 3.0)
    root = math.sqrt(radius_scale) * sixth
    radius = radius_scale * inv
    denom = two_a * root * (b1 + root * (b2 + root * (b3 + root * b4)))
    root_slope = two_a * (0.5 * b1 + root * (b2 + root * (1.5 * b3 + root * (2.0 * b4))))
    recip = 1.0 / (denom * (denom + 1.0))
    log_term = jnp.log(1.0 + recip * (denom + 1.0))
    linear = two_a * (1.0 + correlation_alpha * radius)
    uniform = -linear * log_term
    rho_uniform = (1.0 / 3.0) * (
        (two_a * correlation_alpha) * radius * log_term - linear * recip * (root * root_slope)
    )
    ratio = beta_value / gamma_value
    t_scale = math.pi / (16.0 * (3.0 * math.pi**2) ** (1.0 / 3.0))
    t_square = t_scale * scaled_sigma * (inv2 * inv)
    coefficient = ratio / (jnp.exp(uniform * (-1.0 / gamma_value)) - 1.0)
    u = coefficient * t_square
    inv_d = 1.0 / (1.0 + u + u * u)
    inside = 1.0 + ratio * t_square * (1.0 + u) * inv_d
    gradient = gamma_value * jnp.log(inside)
    common = beta_value * inv_d * (inv_d / inside)
    h_t = common * (1.0 + 2.0 * u)
    h_uniform = -common * (u * u) * (2.0 + u) * t_square * (
        1.0 / gamma_value + coefficient * (1.0 / beta_value)
    )
    d_rho = (
        x_rho
        + uniform
        + gradient
        + rho_uniform * (1.0 + h_uniform)
        - (7.0 / 3.0) * h_t * t_square
    )
    two_d_sigma = inv4 * ((2.0 * exchange * s_scale) * steep + (2.0 * t_scale) * h_t)
    return d_rho, two_d_sigma


def potential_body(
    flag_ref, below_ref, rho_ref, above_ref, head_ref, tail_ref, out_ref,
    ext_ref, part_ref, smooth_ref, flat_ref, fx_ref, fy_ref, fz_ref,
):
    depth, rows, width = out_ref.shape
    total = depth + 2 * reach
    first, last = flag_ref[0] == 1, flag_ref[1] == 1
    slope = 1.0 / (2.0 * grid_step)
    tiles = rows // 8 + 1

    for z in range(total):
        if z < reach:
            plane = below_ref[z]
        elif z < depth + reach:
            plane = rho_ref[z - reach]
        else:
            plane = above_ref[z - depth - reach]
        side = slice(reach * z, reach * (z + 1))
        ext_ref[z, lead : lead + rows] = plane
        ext_ref[z, lead - reach : lead] = head_ref[side]
        ext_ref[z, lead + rows : lead + rows + reach] = tail_ref[side]

    @pl.when(first)
    def _():
        ext_ref[reach - 1] = ext_ref[reach]

    @pl.when(last)
    def _():
        ext_ref[depth + reach] = ext_ref[depth + reach - 1]

    def filter_plane(z, carry):
        for t in range(tiles):
            r = lead - 2 + 8 * t
            along_y = 0.25 * (ext_ref[z, r - 1 : r + 7] + ext_ref[z, r + 1 : r + 9]) + 0.5 * (
                ext_ref[z, r : r + 8]
            )
            part_ref[z, r : r + 8] = (
                0.25 * (roll_x(along_y, 1) + roll_x(along_y, -1)) + 0.5 * along_y
            )
        return carry

    lax.fori_loop(0, total, filter_plane, 0)

    def filter_depth(z, carry):
        r = slice(lead - 2, lead - 2 + 8 * tiles)
        smooth_ref[z, r] = 0.25 * (part_ref[z, r] + part_ref[z + 2, r]) + 0.5 * part_ref[z + 1, r]
        return carry

    lax.fori_loop(0, total - 2, filter_depth, 0)

    @pl.when(first)
    def _():
        smooth_ref[1] = smooth_ref[2]

    @pl.when(last)
    def _():
        smooth_ref[depth + 2] = smooth_ref[depth + 1]

    def local_terms(z, carry):
        for t in range(tiles):
            r = lead - 1 + 8 * t
            center = smooth_ref[z + 1, r : r + 8]
            gx = (roll_x(center, -1) - roll_x(center, 1)) * slope
            gy = (smooth_ref[z + 1, r + 1 : r + 9] - smooth_ref[z + 1, r - 1 : r + 7]) * slope
            gz = (smooth_ref[z + 2, r : r + 8] - smooth_ref[z, r : r + 8]) * slope
            d_rho, two_d_sigma = energy_slopes(center, gx * gx + gy * gy + gz * gz)
            flat_ref[z, r : r + 8] = d_rho
            fx_ref[z, r : r + 8] = two_d_sigma * gx
            fy_ref[z, r : r + 8] = two_d_sigma * gy
            fz_ref[z, r : r + 8] = two_d_sigma * gz
        return carry

    lax.fori_loop(0, depth + 2, local_terms, 0)

    @pl.when(first)
    def _():
        fz_ref[0] = fz_ref[1]

    @pl.when(last)
    def _():
        fz_ref[depth + 1] = fz_ref[depth]

    def collect(z, carry):
        for t in range(rows // 8):
            r = lead + 8 * t
            here = slice(r, r + 8)
            fx = fx_ref[z + 1, here]
            along_x = (roll_x(fx, -1) - roll_x(fx, 1)) * slope
            along_y = (fy_ref[z + 1, r + 1 : r + 9] - fy_ref[z + 1, r - 1 : r + 7]) * slope
            along_z = (fz_ref[z + 2, here] - fz_ref[z, here]) * slope
            out_ref[z, 8 * t : 8 * t + 8] = flat_ref[z + 1, here] - (along_x + along_y + along_z)
        return carry

    lax.fori_loop(0, depth, collect, 0)


def potential_of(flags, below, density, above, head, tail):
    depth, rows, width = density.shape
    tall = -(-(rows + lead + 8) // 8) * 8
    planes = lambda count: pltpu.VMEM((count, tall, width), f32)
    vmem = pl.BlockSpec(memory_space=pltpu.VMEM)
    return call(
        potential_body,
        jax.ShapeDtypeStruct((depth, rows, width), f32),
        56,
        in_specs=[pl.BlockSpec(memory_space=pltpu.SMEM)] + [vmem] * 5,
        out_specs=vmem,
        scratch_shapes=[
            planes(depth + 6), planes(depth + 6), planes(depth + 4),
            planes(depth + 2), planes(depth + 2), planes(depth + 2), planes(depth + 2),
        ],
        name="potential",
    )(flags, below, density, above, head, tail)


def forward_columns_body(x_ref, ch_ref, cl_ref, sh_ref, sl_ref, out_ref, high_ref, low_ref):
    rows = high_ref.shape[0]
    high_ref[...], low_ref[...] = split(x_ref[...].reshape(rows, x_ref.shape[2]))
    group = 4
    block = out_ref.shape[2]

    def step(m, carry):
        at = pl.ds(pl.multiple_of(m * group * block, group * block), group * block)
        to = pl.ds(m * group, group)
        high, low = high_ref[...], low_ref[...]
        out_re = triple(dot_nt, ch_ref[at], cl_ref[at], high, low)
        out_im = -triple(dot_nt, sh_ref[at], sl_ref[at], high, low)
        out_ref[to, 0] = out_re.reshape(group, block, rows)
        out_ref[to, 1] = out_im.reshape(group, block, rows)
        return carry

    lax.fori_loop(0, out_ref.shape[0] // group, step, 0)


def forward_columns(potential, tables, parts, steps):
    depth, local, width = potential.shape
    planes = depth // steps
    block = width // parts
    rows = planes * local
    return call(
        forward_columns_body,
        jax.ShapeDtypeStruct((parts, 2, block, depth * local), f32),
        48,
        grid=(steps,),
        in_specs=[pl.BlockSpec((planes, local, width), lambda i: (i, 0, 0))]
        + [whole((width, width))] * 4,
        out_specs=pl.BlockSpec((parts, 2, block, rows), lambda i: (0, 0, 0, i)),
        scratch_shapes=[pltpu.VMEM((rows, width), bf16), pltpu.VMEM((rows, width), bf16)],
        name="forward_columns",
    )(potential, *tables)


def forward_rows_body(flag_ref, in_ref, ch_ref, cl_ref, sh_ref, sl_ref, out_ref, high_ref, low_ref):
    gather_blocks(in_ref, high_ref, low_ref)
    _, planes, rows, width = out_ref.shape
    group = planes // 2

    def step(m, carry):
        at = pl.ds(pl.multiple_of(m * group * rows, group * rows), group * rows)
        to = pl.ds(m * group, group)
        real = (high_ref[0, at], low_ref[0, at])
        imag = (high_ref[1, at], low_ref[1, at])
        cos = (ch_ref[...], cl_ref[...])
        sin = (sh_ref[...], sl_ref[...])
        out_re = triple(dot_nn, *real, *cos) + triple(dot_nn, *imag, *sin)
        out_ref[0, to] = out_re.reshape(group, rows, width)
        out_im = triple(dot_nn, *imag, *cos) - triple(dot_nn, *real, *sin)
        out_ref[1, to] = out_im.reshape(group, rows, width)
        return carry

    lax.fori_loop(0, 2, step, 0)

    @pl.when(flag_ref[2] == 1)
    def _():
        tile = (8, 128)
        at_zero = (lax.broadcasted_iota(jnp.int32, tile, 0) == 0) & (
            lax.broadcasted_iota(jnp.int32, tile, 1) == 0
        )
        for c in range(2):
            for z in range(planes):
                out_ref[c, z, :8, :128] = jnp.where(at_zero, 0.0, out_ref[c, z, :8, :128])


def forward_rows(flags, blocks, tables, steps):
    parts, _, rows, lanes = blocks.shape
    width = tables[0].shape[0]
    depth = lanes * parts // width
    planes = depth // steps
    scratch = pltpu.VMEM((2, planes * rows, width), bf16)
    return call(
        forward_rows_body,
        jax.ShapeDtypeStruct((2, depth, rows, width), f32),
        48,
        grid=(steps,),
        in_specs=[
            pl.BlockSpec(memory_space=pltpu.SMEM),
            pl.BlockSpec((parts, 2, rows, lanes // steps), lambda i: (0, 0, 0, i)),
        ]
        + [whole((width, width))] * 4,
        out_specs=pl.BlockSpec((2, planes, rows, width), lambda i: (0, i, 0, 0)),
        scratch_shapes=[scratch, scratch],
        name="forward_rows",
    )(flags, blocks, *tables)


def on_device(rho_hat):
    parts = lax.axis_size("py")
    place_z, place_y = lax.axis_index("px"), lax.axis_index("py")
    flags = jnp.stack(
        [place_z == 0, place_z == lax.axis_size("px") - 1, place_y == 0]
    ).astype(jnp.int32)
    width = rho_hat.shape[3]
    tables = phase_tables(width, width // parts)
    columns = inverse_rows(rho_hat, tables, parts, 2)
    columns = lax.all_to_all(columns, "py", 0, 0, tiled=True)
    density = inverse_columns(columns, tables, 2)
    below = shift(density[-reach:], "px", True)
    above = shift(density[:reach], "px", False)
    head, tail = edges(below, density, above)
    head, tail = shift(tail, "py", True), shift(head, "py", False)
    potential = potential_of(flags, below, density, above, head, tail)
    spectral = forward_columns(potential, tables, parts, 2)
    spectral = lax.all_to_all(spectral, "py", 0, 0, tiled=True)
    return forward_rows(flags, spectral, tables, 2)


def solution(mesh):
    return jax.shard_map(
        on_device,
        mesh=mesh,
        in_specs=(P(None, "px", "py", None),),
        out_specs=P(None, "px", "py", None),
        check_vma=False,
    )
```

time: 655 us -> 254 us (0.39)
  the two profiles are of different devices: /device:TPU:14 before, /device:TPU:1 now
where the time goes in v1:
time: 254 us
  blocking collectives  125 us (49%)
  Pallas kernels  96.9 us (38%)
  waiting for transfers between devices  18.8 us (7%)
  starting transfers between devices  7.92 us (3%)
  local copies, waits for them, and re-layouts  4.74 us (2%)
    all_to_all x1, blocking collectives, on_device(): spectral = lax.all_to_all(spectral, 'py', 0, 0, tiled=True)  62.4 us
    all_to_all x1, blocking collectives, on_device(): columns = lax.all_to_all(columns, 'py', 0, 0, tiled=True)  62.3 us
    pallas_call x1, Pallas kernels, potential_of(): call(potential_body, jax.ShapeDtypeStruct((depth, rows, width), f32), 56,...  26.7 us
    pallas_call x1, Pallas kernels, inverse_rows(): call(inverse_rows_body, jax.ShapeDtypeStruct((parts, 2, block, depth * lo...  23.4 us
    ppermute x4, waiting for transfers between devices, shift(): lax.ppermute(value, axis, pairs if up else [(b, a) for a, b in pairs])  18.8 us
    pallas_call x1, Pallas kernels, forward_rows(): call(forward_rows_body, jax.ShapeDtypeStruct((2, depth, rows, width), f32...  18.5 us
    pallas_call x1, Pallas kernels, forward_columns(): call(forward_columns_body, jax.ShapeDtypeStruct((parts, 2, block, depth *...  13.2 us
    pallas_call x1, Pallas kernels, inverse_columns(): call(inverse_columns_body, jax.ShapeDtypeStruct((depth, rows, width), f32...  13 us
  transfers between devices with their start and end apart: 4, of which 4 were waited for; matrix products, arithmetic and copies ran while one was open for 0% of the time, Pallas kernels for 0%

profile of v1, /device:TPU:1, one launch (start us, length us, event | category | flops | bytes accessed | tf_op | source)
XLA Modules:
  0.0 253.7 jit_solution(1437955340735915216)
XLA Ops:
  0.0 1.0 copy-done.5
  1.0 0.9 copy-done.6
  1.9 1.1 tables.1
  3.0 0.0 copy-start.1
  3.0 23.4 %inverse_rows.1 = f32[16,2,48,768]{3,2,1,0:T(8,128)} custom-call(f32[2,16,48,768]{3,2,1,0:T(8,128)} %x_ref.1, bf16[768,768]{1,0:T(8,128)(2,1)S(1)} %get-tuple-element.11.ch_ref, bf16[768,768]{1,0:T(8,128)(2,1)S(1)} %get-tuple-element.12.cl_ref, bf16[768,768]{1,0:T(8,128)(2,1)S(1)} %get-tuple-element.13.sh_ref, bf16[768,768]{1,0:T(8,128)(2,1)S(1)} %get-tuple-element.14.sl_ref), custom_call_target="tpu_custom_call" | custom-call | tf_op jit(solution)/shard_map/inverse_rows/pallas_call | solution.py:106
  26.4 62.3 %all_to_all.10.in_ref = f32[16,2,48,768]{3,2,1,0:T(8,128)} all-to-all(f32[16,2,48,768]{3,2,1,0:T(8,128)} %inverse_rows.1), channel_id=1, replica_groups=mesh['px'=8,'py'=16] {'py'}, dimensions={0} | all-to-all | bytes 9437184 | tf_op jit(solution)/shard_map/all_to_all | solution.py:473
  88.7 0.0 copy-done.1
  88.7 13.0 %inverse_columns.1.first_ref.last_ref.rho_ref = f32[16,48,768]{2,1,0:T(8,128)} custom-call(f32[16,2,48,768]{3,2,1,0:T(8,128)} %all_to_all.10.in_ref, bf16[768,768]{1,0:T(8,128)(2,1)S(1)} %get-tuple-element.11.ch_ref, bf16[768,768]{1,0:T(8,128)(2,1)S(1)} %get-tuple-element.12.cl_ref, bf16[768,768]{1,0:T(8,128)(2,1)S(1)} %get-tuple-element.13.sh_ref, ...), custom_call_target="tpu_custom_call" | custom-call | tf_op jit(solution)/shard_map/inverse_columns/pallas_call | solution.py:153
  101.6 1.2 fusion
  102.8 5.6 %collective-permute-start.1 = (f32[3,48,768]{2,1,0:T(8,128)S(1)}, f32[3,48,768]{2,1,0:T(8,128)S(1)}, u32[]{:S(2)}, u32[]{:S(2)}) collective-permute-start(f32[3,48,768]{2,1,0:T(8,128)S(1)} %get-tuple-element.17), channel_id=1, source_target_pairs={{16,0},{32,16},{48,32},{64,48},{80,64},{96,80},{112,96},{0,112},{1... | collective-permute-start | bytes 1327112 | tf_op jit(solution)/shard_map/ppermute | solution.py:169
  108.4 0.0 collective-permute-start
  108.4 8.4 %collective-permute-done.1.high_ref.above_ref = f32[3,48,768]{2,1,0:T(8,128)S(1)} collective-permute-done((f32[3,48,768]{2,1,0:T(8,128)S(1)}, f32[3,48,768]{2,1,0:T(8,128)S(1)}, u32[]{:S(2)}, u32[]{:S(2)}) %collective-permute-start.1) | collective-permute-done | bytes 442400 | tf_op jit(solution)/shard_map/ppermute | solution.py:169
  116.8 5.5 %collective-permute-done.low_ref.below_ref = f32[3,48,768]{2,1,0:T(8,128)S(1)} collective-permute-done((f32[3,48,768]{2,1,0:T(8,128)S(1)}, f32[3,48,768]{2,1,0:T(8,128)S(1)}, u32[]{:S(2)}, u32[]{:S(2)}) %collective-permute-start) | collective-permute-done | bytes 442400 | tf_op jit(solution)/shard_map/ppermute | solution.py:169
  122.3 1.7 copy-done
  124.0 0.9 edges.1
  124.9 1.9 collective-permute-start.2
  126.8 0.5 collective-permute-start.3
  127.3 0.6 add_convert_fusion.flag_ref
  127.9 2.1 collective-permute-done.2.head_ref
  130.0 2.8 %collective-permute-done.3.tail_ref = f32[72,768]{1,0:T(8,128)} collective-permute-done((f32[72,768]{1,0:T(8,128)}, f32[72,768]{1,0:T(8,128)}, u32[]{:S(2)}, u32[]{:S(2)}) %collective-permute-start.3) | collective-permute-done | bytes 221216 | tf_op jit(solution)/shard_map/ppermute | solution.py:169
  132.8 26.7 %potential.1.x_ref = f32[16,48,768]{2,1,0:T(8,128)} custom-call(s32[3]{0:T(128)} %add_convert_fusion.flag_ref, f32[3,48,768]{2,1,0:T(8,128)} %copy-done.4, f32[16,48,768]{2,1,0:T(8,128)} %inverse_columns.1.first_ref.last_ref.rho_ref, f32[3,48,768]{2,1,0:T(8,128)} %copy-done.3, f32[72,768]{1,0:T(8,128)} %collective-permute-done.2.head_ref, ...), custom_call_target="tpu_custom_call" | custom-call | tf_op jit(solution)/shard_map/potential/pallas_call | solution.py:360
  159.5 13.2 %forward_columns.1 = f32[16,2,48,768]{3,2,1,0:T(8,128)} custom-call(f32[16,48,768]{2,1,0:T(8,128)} %potential.1.x_ref, bf16[768,768]{1,0:T(8,128)(2,1)S(1)} %get-tuple-element.11.ch_ref, bf16[768,768]{1,0:T(8,128)(2,1)S(1)} %get-tuple-element.12.cl_ref, bf16[768,768]{1,0:T(8,128)(2,1)S(1)} %get-tuple-element.13.sh_ref, bf16[768,768]{1,0:T(8,128)(2,1)S(1)} %copy-done.2), custom_call_target="tpu_custom_call" | custom-call | tf_op jit(solution)/shard_map/forward_columns/pallas_call | solution.py:398
  172.8 62.4 %all_to_all.11.in_ref = f32[16,2,48,768]{3,2,1,0:T(8,128)} all-to-all(f32[16,2,48,768]{3,2,1,0:T(8,128)} %forward_columns.1), channel_id=1, replica_groups=mesh['px'=8,'py'=16] {'py'}, dimensions={0} | all-to-all | bytes 9437184 | tf_op jit(solution)/shard_map/all_to_all | solution.py:481
  235.2 18.5 %forward_rows.1 = f32[2,16,48,768]{3,2,1,0:T(8,128)} custom-call(s32[3]{0:T(128)S(1)} %copy-done.7, f32[16,2,48,768]{3,2,1,0:T(8,128)} %all_to_all.11.in_ref, bf16[768,768]{1,0:T(8,128)(2,1)S(1)} %get-tuple-element.11.ch_ref, bf16[768,768]{1,0:T(8,128)(2,1)S(1)} %get-tuple-element.12.cl_ref, bf16[768,768]{1,0:T(8,128)(2,1)S(1)} %get-tuple-element.13.sh_ref, ...), custom_call_target="tpu_custom_call" | custom-call | tf_op jit(solution)/shard_map/forward_rows/pallas_call | solution.py:448
  (11 shorter events, 0.0 us)
Async XLA Ops:
  0.0 1.0 copy-start.5
  1.0 0.9 copy-start.6
  3.0 85.7 %copy-start.1 = (bf16[768,768]{1,0:T(8,128)(2,1)}, bf16[768,768]{1,0:T(8,128)(2,1)S(1)}, u32[]{:S(2)}) copy-start(bf16[768,768]{1,0:T(8,128)(2,1)S(1)} %get-tuple-element.14.sl_ref) | copy-start | bytes 3538948
  102.8 14.0 %collective-permute-start.1 = (f32[3,48,768]{2,1,0:T(8,128)S(1)}, f32[3,48,768]{2,1,0:T(8,128)S(1)}, u32[]{:S(2)}, u32[]{:S(2)}) collective-permute-start(f32[3,48,768]{2,1,0:T(8,128)S(1)} %get-tuple-element.17), channel_id=1, source_target_pairs={{16,0},{32,16},{48,32},{64,48},{80,64},{96,80},{112,96},{0,112},{1... | collective-permute-start | bytes 1327112 | tf_op jit(solution)/shard_map/ppermute | solution.py:169
  108.4 13.9 %collective-permute-start = (f32[3,48,768]{2,1,0:T(8,128)S(1)}, f32[3,48,768]{2,1,0:T(8,128)S(1)}, u32[]{:S(2)}, u32[]{:S(2)}) collective-permute-start(f32[3,48,768]{2,1,0:T(8,128)S(1)} %get-tuple-element.18), channel_id=1, source_target_pairs={{0,16},{16,32},{32,48},{48,64},{64,80},{80,96},{96,112},{112,0},{1... | collective-permute-start | bytes 1327112 | tf_op jit(solution)/shard_map/ppermute | solution.py:169
  116.8 8.2 %copy-start.3 = (f32[3,48,768]{2,1,0:T(8,128)}, f32[3,48,768]{2,1,0:T(8,128)S(1)}, u32[]{:S(2)}) copy-start(f32[3,48,768]{2,1,0:T(8,128)S(1)} %collective-permute-done.1.high_ref.above_ref) | copy-start | bytes 1327108
  122.3 1.7 copy-start
  124.0 1.0 copy-start.4
  124.9 5.1 %collective-permute-start.2 = (f32[72,768]{1,0:T(8,128)}, f32[72,768]{1,0:T(8,128)}, u32[]{:S(2)}, u32[]{:S(2)}) collective-permute-start(f32[72,768]{1,0:T(8,128)} %get-tuple-element.15), channel_id=1, source_target_pairs={{0,1},{1,2},{2,3},{3,4},{4,5},{5,6},{6,7},{7,8},{8,9},{9,10},{10,1... | collective-permute-start | bytes 663560 | tf_op jit(solution)/shard_map/ppermute | solution.py:169
  126.8 6.0 %collective-permute-start.3 = (f32[72,768]{1,0:T(8,128)}, f32[72,768]{1,0:T(8,128)}, u32[]{:S(2)}, u32[]{:S(2)}) collective-permute-start(f32[72,768]{1,0:T(8,128)} %get-tuple-element.16), channel_id=1, source_target_pairs={{1,0},{2,1},{3,2},{4,3},{5,4},{6,5},{7,6},{8,7},{9,8},{10,9},{11,1... | collective-permute-start | bytes 663560 | tf_op jit(solution)/shard_map/ppermute | solution.py:169
  127.9 31.6 %copy-start.2 = (bf16[768,768]{1,0:T(8,128)(2,1)S(1)}, bf16[768,768]{1,0:T(8,128)(2,1)}, u32[]{:S(2)}) copy-start(bf16[768,768]{1,0:T(8,128)(2,1)} %copy-done.1) | copy-start | bytes 3538948
  172.8 62.4 %copy-start.7 = (s32[3]{0:T(128)S(1)}, s32[3]{0:T(128)}, u32[]{:S(2)}) copy-start(s32[3]{0:T(128)} %add_convert_fusion.flag_ref) | copy-start | bytes 40

commit v2 on v1

v2 whole, which is shorter than its diff:
```python
import math

import jax
import jax.numpy as jnp
import numpy as np
from jax import lax
from jax.experimental import pallas as pl
from jax.experimental.pallas import tpu as pltpu
from jax.sharding import PartitionSpec as P

grid_step = 0.25
density_floor = 0.02
density_scale = 0.2
kappa_value = 0.804
mu_value = 0.2195149727645171
beta_value = 0.06672455060314922
gamma_value = (1.0 - math.log(2.0)) / (math.pi * math.pi)
correlation_scale = 0.031091
correlation_alpha = 0.2137
correlation_terms = (7.5957, 3.5876, 1.6382, 0.49294)

f32 = jnp.float32
bf16 = jnp.bfloat16
reach = 3
lead = 9


def params(mib):
    return pltpu.CompilerParams(vmem_limit_bytes=mib << 20)


def call(body, out, mib, cost, **options):
    estimate = pl.CostEstimate(flops=int(cost * 1e9), bytes_accessed=1 << 20, transcendentals=0)
    return pl.pallas_call(
        body, out_shape=out, compiler_params=params(mib), cost_estimate=estimate, **options
    )


def array(*shape):
    return jax.ShapeDtypeStruct(shape, f32)


def whole(shape):
    return pl.BlockSpec(shape, lambda *_: (0,) * len(shape))


def split(value):
    high = value.astype(bf16)
    return high, (value - high.astype(f32)).astype(bf16)


def dot_nt(left, right):
    return lax.dot_general(left, right, (((1,), (1,)), ((), ())), preferred_element_type=f32)


def dot_nn(left, right):
    return lax.dot_general(left, right, (((1,), (0,)), ((), ())), preferred_element_type=f32)


def triple(dot, left_high, left_low, right_high, right_low):
    return dot(left_high, right_high) + (dot(left_low, right_high) + dot(left_high, right_low))


def tables_body(stride, coarse_ref, fine_ref, ch_ref, cl_ref, sh_ref, sl_ref):
    fine_cos, fine_sin = fine_ref[0], fine_ref[1]
    for a in range(coarse_ref.shape[1]):
        cos_a, sin_a = coarse_ref[0, a : a + 1], coarse_ref[1, a : a + 1]
        rows = slice(stride * a, stride * (a + 1))
        ch_ref[rows], cl_ref[rows] = split(cos_a * fine_cos - sin_a * fine_sin)
        sh_ref[rows], sl_ref[rows] = split(sin_a * fine_cos + cos_a * fine_sin)


def phase_tables(length, stride):
    def waves(rows, scale):
        angle = (np.outer(rows, np.arange(length)) % length) * (2.0 * math.pi / length)
        return np.stack([np.cos(angle), np.sin(angle)]).astype(np.float32) * np.float32(scale)

    coarse = waves(np.arange(0, length, stride), 1.0)
    fine = waves(np.arange(stride), 1.0 / math.sqrt(length))
    out = [jax.ShapeDtypeStruct((length, length), bf16)] * 4
    body = lambda *refs: tables_body(stride, *refs)
    return call(body, out, 32, 2, name="tables")(jnp.asarray(coarse), jnp.asarray(fine))


def inverse_rows_body(count, *refs):
    planes, (ch_ref, cl_ref, sh_ref, sl_ref, out_ref, wide_ref) = refs[:count], refs[count:]
    width = ch_ref.shape[0]
    lanes = wide_ref.shape[1] // 2
    for c in range(2):
        joined = jnp.concatenate([ref[c].reshape(-1, width) for ref in planes], axis=0)
        high, low = split(joined.T)
        cos_at = slice(c * lanes, (c + 1) * lanes)
        sin_at = slice((1 - c) * lanes, (2 - c) * lanes)
        for k, value in enumerate((high, high, low)):
            wide_ref[k * width : (k + 1) * width, cos_at] = value
            wide_ref[(k + 3) * width : (k + 4) * width, sin_at] = value if c == 0 else -value
    _, block, out_lanes = out_ref.shape
    group = out_ref.shape[0] // 2

    def step(m, carry):
        at = pl.ds(pl.multiple_of(m * group * block, group * block), group * block)
        ch, sh = ch_ref[at], sh_ref[at]
        left = jnp.concatenate([ch, cl_ref[at], ch, sh, sl_ref[at], sh], axis=1)
        product = dot_nn(left, wide_ref[...])
        out_ref[pl.ds(m * group, group)] = product.reshape(group, block, out_lanes)
        return carry

    lax.fori_loop(0, 2, step, 0)


def inverse_rows(rho_hat, tables, parts, blocks):
    _, depth, local, width = rho_hat.shape
    unit = depth // 4
    lanes = len(blocks) * unit * local
    piece = lambda b: pl.BlockSpec((2, unit, local, width), lambda i: (0, b, 0, 0))
    out = (parts, width // parts, 2 * lanes)
    return call(
        lambda *refs: inverse_rows_body(len(blocks), *refs),
        array(*out),
        48,
        5.0 * len(blocks),
        grid=(1,),
        in_specs=[piece(b) for b in blocks] + [whole((width, width))] * 4,
        out_specs=whole(out),
        scratch_shapes=[pltpu.VMEM((6 * width, 2 * lanes), bf16)],
        name="inverse_rows",
    )(*[rho_hat] * len(blocks), *tables)


def gather_blocks(in_ref, high_ref, low_ref, total, start, count):
    parts, rows, _ = in_ref.shape
    local = high_ref.shape[2] // parts
    for z in range(count):
        to = slice(z * rows, (z + 1) * rows)
        for c in range(2):
            first = (c * total + start + z) * local
            pieces = [in_ref[s, :, first : first + local] for s in range(parts)]
            high_ref[c, to], low_ref[c, to] = split(jnp.concatenate(pieces, axis=-1))


def inverse_columns_body(
    in_ref, ch_ref, cl_ref, sh_ref, sl_ref, out_ref, head_ref, tail_ref, high_ref, low_ref
):
    planes, rows, width = out_ref.shape
    gather_blocks(in_ref, high_ref, low_ref, planes, 0, planes)
    field = triple(dot_nn, high_ref[0], low_ref[0], ch_ref[...], cl_ref[...])
    field = field - triple(dot_nn, high_ref[1], low_ref[1], sh_ref[...], sl_ref[...])
    soft = jnp.maximum(field, 0.0) + jnp.log1p(jnp.exp(-jnp.abs(field)))
    out_ref[...] = (density_floor + density_scale * soft).reshape(planes, rows, width)
    for z in range(planes):
        at = slice(reach * z, reach * (z + 1))
        head_ref[at] = out_ref[z, :reach]
        tail_ref[at] = out_ref[z, rows - reach :]


def inverse_columns(blocks, tables):
    parts, rows, lanes = blocks.shape
    width = tables[0].shape[0]
    planes = lanes * parts // (2 * width)
    scratch = pltpu.VMEM((2, planes * rows, width), bf16)
    side = (reach * planes, width)
    return call(
        inverse_columns_body,
        [array(planes, rows, width), array(*side), array(*side)],
        48,
        1.2 * planes,
        grid=(1,),
        in_specs=[whole(blocks.shape)] + [whole((width, width))] * 4,
        out_specs=[whole((planes, rows, width)), whole(side), whole(side)],
        scratch_shapes=[scratch, scratch],
        name="inverse_columns",
    )(blocks, *tables)


def shift(value, axis, up):
    count = lax.axis_size(axis)
    pairs = [(i, (i + 1) % count) for i in range(count)]
    return lax.ppermute(value, axis, pairs if up else [(b, a) for a, b in pairs])


def edges_body(below_ref, head_ref, tail_ref, above_ref, head_out, tail_out):
    rows = below_ref.shape[1]
    middle = head_ref.shape[0]
    for z in range(reach):
        for ref, first in ((below_ref, 0), (above_ref, reach * reach + middle)):
            to = slice(first + reach * z, first + reach * (z + 1))
            head_out[to], tail_out[to] = ref[z, :reach], ref[z, rows - reach :]
    to = slice(reach * reach, reach * reach + middle)
    head_out[to], tail_out[to] = head_ref[...], tail_ref[...]


def edges(below, head, tail, above):
    width = head.shape[1]
    count = -(-(head.shape[0] + 2 * reach * reach) // 8) * 8
    vmem = pl.BlockSpec(memory_space=pltpu.VMEM)
    return call(
        edges_body,
        [array(count, width)] * 2,
        16,
        1.0,
        in_specs=[vmem] * 4,
        out_specs=[vmem] * 2,
        name="edges",
    )(below, head, tail, above)


def roll_x(value, by):
    return pltpu.roll(value, by % value.shape[-1], value.ndim - 1)


def energy_slopes(rho, sigma):
    two_a = 2.0 * correlation_scale
    b1, b2, b3, b4 = correlation_terms
    sixth = jnp.exp(jnp.log(rho) * (-1.0 / 6.0))
    inv = sixth * sixth
    inv2 = inv * inv
    inv4 = inv2 * inv2
    cube = rho * inv2
    exchange = -0.75 * (3.0 / math.pi) ** (1.0 / 3.0)
    s_scale = 0.25 / (3.0 * math.pi**2) ** (2.0 / 3.0)
    scaled_sigma = sigma * inv4
    s_square = s_scale * scaled_sigma * inv4
    weight = 1.0 / (1.0 + (mu_value / kappa_value) * s_square)
    enhance = (1.0 + kappa_value) - kappa_value * weight
    steep = mu_value * weight * weight
    x_rho = (exchange * cube) * ((4.0 / 3.0) * enhance - (8.0 / 3.0) * steep * s_square)
    radius_scale = (3.0 / (4.0 * math.pi)) ** (1.0 / 3.0)
    root = math.sqrt(radius_scale) * sixth
    radius = radius_scale * inv
    denom = two_a * root * (b1 + root * (b2 + root * (b3 + root * b4)))
    root_slope = two_a * (0.5 * b1 + root * (b2 + root * (1.5 * b3 + root * (2.0 * b4))))
    recip = 1.0 / (denom * (denom + 1.0))
    log_term = jnp.log(1.0 + recip * (denom + 1.0))
    linear = two_a * (1.0 + correlation_alpha * radius)
    uniform = -linear * log_term
    rho_uniform = (1.0 / 3.0) * (
        (two_a * correlation_alpha) * radius * log_term - linear * recip * (root * root_slope)
    )
    ratio = beta_value / gamma_value
    t_scale = math.pi / (16.0 * (3.0 * math.pi**2) ** (1.0 / 3.0))
    t_square = t_scale * scaled_sigma * (inv2 * inv)
    coefficient = ratio / (jnp.exp(uniform * (-1.0 / gamma_value)) - 1.0)
    u = coefficient * t_square
    inv_d = 1.0 / (1.0 + u + u * u)
    inside = 1.0 + ratio * t_square * (1.0 + u) * inv_d
    gradient = gamma_value * jnp.log(inside)
    common = beta_value * inv_d * (inv_d / inside)
    h_t = common * (1.0 + 2.0 * u)
    h_uniform = -common * (u * u) * (2.0 + u) * t_square * (
        1.0 / gamma_value + coefficient * (1.0 / beta_value)
    )
    d_rho = (
        x_rho
        + uniform
        + gradient
        + rho_uniform * (1.0 + h_uniform)
        - (7.0 / 3.0) * h_t * t_square
    )
    two_d_sigma = inv4 * ((2.0 * exchange * s_scale) * steep + (2.0 * t_scale) * h_t)
    return d_rho, two_d_sigma


def potential_body(sources, bottom, top, flag_ref, *refs):
    out_ref, ext_ref, part_ref, smooth_ref, flat_ref, fx_ref, fy_ref, fz_ref = refs[-8:]
    depth, rows, width = out_ref.shape
    total = depth + 2 * reach
    slope = 1.0 / (2.0 * grid_step)
    tiles = rows // 8 + 1

    def at_end(is_end, flag):
        return pl.when(flag_ref[flag] == 1) if is_end else lambda body: None

    for z, (plane, at, side, row) in enumerate(sources):
        ext_ref[z, lead : lead + rows] = refs[plane][at]
        ext_ref[z, lead - reach : lead] = refs[side][row : row + reach]
        ext_ref[z, lead + rows : lead + rows + reach] = refs[side + 1][row : row + reach]

    @at_end(bottom, 0)
    def _():
        ext_ref[reach - 1] = ext_ref[reach]

    @at_end(top, 1)
    def _():
        ext_ref[depth + reach] = ext_ref[depth + reach - 1]

    def filter_plane(z, carry):
        for t in range(tiles):
            r = lead - 2 + 8 * t
            along_y = 0.25 * (ext_ref[z, r - 1 : r + 7] + ext_ref[z, r + 1 : r + 9]) + 0.5 * (
                ext_ref[z, r : r + 8]
            )
            part_ref[z, r : r + 8] = (
                0.25 * (roll_x(along_y, 1) + roll_x(along_y, -1)) + 0.5 * along_y
            )
        return carry

    lax.fori_loop(0, total, filter_plane, 0)

    def filter_depth(z, carry):
        r = slice(lead - 2, lead - 2 + 8 * tiles)
        smooth_ref[z, r] = 0.25 * (part_ref[z, r] + part_ref[z + 2, r]) + 0.5 * part_ref[z + 1, r]
        return carry

    lax.fori_loop(0, total - 2, filter_depth, 0)

    @at_end(bottom, 0)
    def _():
        smooth_ref[1] = smooth_ref[2]

    @at_end(top, 1)
    def _():
        smooth_ref[depth + 2] = smooth_ref[depth + 1]

    def local_terms(z, carry):
        for t in range(tiles):
            r = lead - 1 + 8 * t
            center = smooth_ref[z + 1, r : r + 8]
            gx = (roll_x(center, -1) - roll_x(center, 1)) * slope
            gy = (smooth_ref[z + 1, r + 1 : r + 9] - smooth_ref[z + 1, r - 1 : r + 7]) * slope
            gz = (smooth_ref[z + 2, r : r + 8] - smooth_ref[z, r : r + 8]) * slope
            d_rho, two_d_sigma = energy_slopes(center, gx * gx + gy * gy + gz * gz)
            flat_ref[z, r : r + 8] = d_rho
            fx_ref[z, r : r + 8] = two_d_sigma * gx
            fy_ref[z, r : r + 8] = two_d_sigma * gy
            fz_ref[z, r : r + 8] = two_d_sigma * gz
        return carry

    lax.fori_loop(0, depth + 2, local_terms, 0)

    @at_end(bottom, 0)
    def _():
        fz_ref[0] = fz_ref[1]

    @at_end(top, 1)
    def _():
        fz_ref[depth + 1] = fz_ref[depth]

    def collect(z, carry):
        for t in range(rows // 8):
            r = lead + 8 * t
            here = slice(r, r + 8)
            fx = fx_ref[z + 1, here]
            along_x = (roll_x(fx, -1) - roll_x(fx, 1)) * slope
            along_y = (fy_ref[z + 1, r + 1 : r + 9] - fy_ref[z + 1, r - 1 : r + 7]) * slope
            along_z = (fz_ref[z + 2, here] - fz_ref[z, here]) * slope
            out_ref[z, 8 * t : 8 * t + 8] = flat_ref[z + 1, here] - (along_x + along_y + along_z)
        return carry

    lax.fori_loop(0, depth, collect, 0)


def potential_of(flags, arrays, sources, start, count, depth):
    _, rows, width = arrays[0].shape
    tall = -(-(rows + lead + 8) // 8) * 8
    planes = lambda extra: pltpu.VMEM((count + extra, tall, width), f32)
    vmem = pl.BlockSpec(memory_space=pltpu.VMEM)
    used = sources[start : start + count + 2 * reach]
    body = lambda *refs: potential_body(used, start == 0, start + count == depth, *refs)
    return call(
        body,
        array(count, rows, width),
        56,
        2.0 * (count + 2),
        in_specs=[pl.BlockSpec(memory_space=pltpu.SMEM)] + [vmem] * len(arrays),
        out_specs=vmem,
        scratch_shapes=[planes(extra) for extra in (6, 6, 4, 2, 2, 2, 2)],
        name="potential",
    )(flags, *arrays)


def forward_columns_body(x_ref, ch_ref, cl_ref, sh_ref, sl_ref, out_ref, tall_ref):
    planes, rows, width = x_ref.shape
    high, low = split(x_ref[...].reshape(planes * rows, width).T)
    for k, value in enumerate((high, high, low)):
        tall_ref[k * width : (k + 1) * width] = value
    _, block, out_lanes = out_ref.shape
    group = out_ref.shape[0] // 2

    def step(m, carry):
        at = pl.ds(pl.multiple_of(m * group * block, group * block), group * block)
        ch, sh = ch_ref[at], sh_ref[at]
        real = dot_nn(jnp.concatenate([ch, cl_ref[at], ch], axis=1), tall_ref[...])
        imag = dot_nn(jnp.concatenate([sh, sl_ref[at], sh], axis=1), tall_ref[...])
        both = jnp.concatenate([real, -imag], axis=1)
        out_ref[pl.ds(m * group, group)] = both.reshape(group, block, out_lanes)
        return carry

    lax.fori_loop(0, 2, step, 0)


def forward_columns(potential, tables, parts):
    planes, rows, width = potential.shape
    lanes = planes * rows
    out = (parts, width // parts, 2 * lanes)
    return call(
        forward_columns_body,
        array(*out),
        48,
        1.2 * planes,
        grid=(1,),
        in_specs=[whole(potential.shape)] + [whole((width, width))] * 4,
        out_specs=whole(out),
        scratch_shapes=[pltpu.VMEM((3 * width, lanes), bf16)],
        name="forward_columns",
    )(potential, *tables)


def forward_rows_body(total, flag_ref, in_ref, *refs):
    ch_ref, cl_ref, sh_ref, sl_ref, out_ref, high_ref, low_ref = refs[-7:]
    _, planes, rows, width = out_ref.shape
    for i in range(total // planes):

        @pl.when(pl.program_id(0) == i)
        def _():
            gather_blocks(in_ref, high_ref, low_ref, total, i * planes, planes)

    real = (high_ref[0], low_ref[0])
    imag = (high_ref[1], low_ref[1])
    cos = (ch_ref[...], cl_ref[...])
    sin = (sh_ref[...], sl_ref[...])
    out_re = triple(dot_nn, *real, *cos) + triple(dot_nn, *imag, *sin)
    out_ref[0] = out_re.reshape(planes, rows, width)
    out_im = triple(dot_nn, *imag, *cos) - triple(dot_nn, *real, *sin)
    out_ref[1] = out_im.reshape(planes, rows, width)

    @pl.when(flag_ref[2] == 1)
    def _():
        tile = (8, 128)
        at_zero = (lax.broadcasted_iota(jnp.int32, tile, 0) == 0) & (
            lax.broadcasted_iota(jnp.int32, tile, 1) == 0
        )
        for c in range(2):
            for z in range(planes):
                out_ref[c, z, :8, :128] = jnp.where(at_zero, 0.0, out_ref[c, z, :8, :128])


def forward_rows(flags, blocks, tables, first, depth, before):
    parts, rows, lanes = blocks.shape
    width = tables[0].shape[0]
    total = lanes * parts // (2 * width)
    unit = depth // 4
    scratch = pltpu.VMEM((2, unit * rows, width), bf16)
    earlier = [] if before is None else [before]
    return call(
        lambda *refs: forward_rows_body(total, *refs),
        array(2, depth, rows, width),
        48,
        2.3 * total,
        grid=(total // unit,),
        in_specs=[pl.BlockSpec(memory_space=pltpu.SMEM), whole(blocks.shape)]
        + [pl.BlockSpec(memory_space=pl.ANY)] * len(earlier)
        + [whole((width, width))] * 4,
        out_specs=pl.BlockSpec((2, unit, rows, width), lambda i: (0, first + i, 0, 0)),
        scratch_shapes=[scratch, scratch],
        input_output_aliases={2: 0} if earlier else {},
        name="forward_rows",
    )(flags, blocks, *earlier, *tables)


def exchange(value):
    return lax.all_to_all(value, "py", 0, 0, tiled=True)


def on_device(rho_hat):
    parts = lax.axis_size("py")
    place_z, place_y = lax.axis_index("px"), lax.axis_index("py")
    flags = jnp.stack(
        [place_z == 0, place_z == lax.axis_size("px") - 1, place_y == 0]
    ).astype(jnp.int32)
    depth, width = rho_hat.shape[1], rho_hat.shape[3]
    unit = depth // 4
    tables = phase_tables(width, width // parts)

    outer = exchange(inverse_rows(rho_hat, tables, parts, (0, 3)))
    inner = exchange(inverse_rows(rho_hat, tables, parts, (1, 2)))
    outer, head, tail = inverse_columns(outer, tables)
    below = shift(outer[-reach:], "px", True)
    above = shift(outer[:reach], "px", False)
    head, tail = edges(below, head, tail, above)
    head, tail = shift(tail, "py", True), shift(head, "py", False)
    inner, inner_head, inner_tail = inverse_columns(inner, tables)
    inner_head, inner_tail = shift(inner_tail, "py", True), shift(inner_head, "py", False)

    arrays = [below, outer, inner, above, head, tail, inner_head, inner_tail]
    sources = []
    for z in range(-reach, depth + reach):
        if z < 0:
            sources.append((0, z + reach, 4, reach * (z + reach)))
        elif z < unit:
            sources.append((1, z, 4, reach * (z + reach)))
        elif z < depth - unit:
            sources.append((2, z - unit, 6, reach * (z - unit)))
        elif z < depth:
            at = z - depth + 2 * unit
            sources.append((1, at, 4, reach * (at + reach)))
        else:
            at = z - depth
            sources.append((3, at, 4, reach * (at + reach + 2 * unit)))

    result = None
    for first, count in ((0, 1), (1, 2), (3, 1)):
        planes = (first * unit, count * unit)
        potential = potential_of(flags, arrays, sources, *planes, depth)
        spectral = exchange(forward_columns(potential, tables, parts))
        result = forward_rows(flags, spectral, tables, first, depth, result)
    return result


def solution(mesh):
    return jax.shard_map(
        on_device,
        mesh=mesh,
        in_specs=(P(None, "px", "py", None),),
        out_specs=P(None, "px", "py", None),
        check_vma=False,
    )
```

time: 254 us -> 237 us (0.933)
  blocking collectives: 125 us -> 0 us
  waiting for transfers between devices: 18.8 us -> 59.5 us
  starting transfers between devices: 7.92 us -> 42.2 us
  local copies, waits for them, and re-layouts: 4.74 us -> 23.9 us
  Pallas kernels: 96.9 us -> 109 us
    all_to_all x2 -> x0, blocking collectives: 125 us -> none  [the longest x1 62.4 us: on_device(): spectral = lax.all_to_all(spectral, 'py', 0, 0, tiled=True)]
    all_to_all x0 -> x5, waiting for transfers between devices: none -> 33.9 us  [exchange(): return lax.all_to_all(value, 'py', 0, 0, tiled=True)]
    all_to_all x0 -> x5, starting transfers between devices: none -> 30.9 us  [exchange(): return lax.all_to_all(value, 'py', 0, 0, tiled=True)]
    unnamed x16 -> x80, local copies, waits for them, and re-layouts: 3.54 us -> 23.8 us
    pallas_call x7 -> x15, Pallas kernels: 96.9 us -> 109 us  [the longest x3 38.8 us: potential_of(): call(body, array(count, rows, width), 56, 2.0 * (count + 2), in_specs=[pl...]
    ppermute x4 -> x6, waiting for transfers between devices: 18.8 us -> 25.7 us  [shift(): lax.ppermute(value, axis, pairs if up else [(b, a) for a, b in pairs])]
    ppermute x4 -> x6, starting transfers between devices: 7.92 us -> 11.3 us  [shift(): lax.ppermute(value, axis, pairs if up else [(b, a) for a, b in pairs])]
  transfers between devices with their start and end apart: 4 -> 11, of which waited for: 4 -> 7; matrix products, arithmetic and copies ran while one was open for 0% -> 0% of each run, Pallas kernels for 0% -> 32%
where the time goes in v2:
time: 237 us; the launch traced here: 236 us
  Pallas kernels  109 us (46%)
  waiting for transfers between devices  59.5 us (25%)
  starting transfers between devices  42.2 us (18%)
  local copies, waits for them, and re-layouts  23.9 us (10%)
    pallas_call x3, Pallas kernels, potential_of(): call(body, array(count, rows, width), 56, 2.0 * (count + 2), in_specs=[pl...  38.8 us
    all_to_all x5, waiting for transfers between devices, exchange(): return lax.all_to_all(value, 'py', 0, 0, tiled=True)  33.9 us
    all_to_all x5, starting transfers between devices, exchange(): return lax.all_to_all(value, 'py', 0, 0, tiled=True)  30.9 us
    ppermute x6, waiting for transfers between devices, shift(): lax.ppermute(value, axis, pairs if up else [(b, a) for a, b in pairs])  25.7 us
    unnamed x80, local copies, waits for them, and re-layouts  23.8 us
    pallas_call x2, Pallas kernels, inverse_rows(): call(lambda *refs: inverse_rows_body(len(blocks), *refs), array(*out), 48...  20.7 us
    pallas_call x3, Pallas kernels, forward_rows(): call(lambda *refs: forward_rows_body(total, *refs), array(2, depth, rows,...  20 us
    pallas_call x3, Pallas kernels, forward_columns(): call(forward_columns_body, array(*out), 48, 1.2 * planes, grid=(1,), in_s...  15.7 us
  transfers between devices with their start and end apart: 11, of which 7 were waited for; matrix products, arithmetic and copies ran while one was open for 0% of the time, Pallas kernels for 32%

profile of v2, /device:TPU:1, one launch (start us, length us, event | category | flops | bytes accessed | tf_op | source)
XLA Modules:
  0.0 235.6 jit_solution(3217838443466360028)
XLA Ops:
  3.0 11.0 %inverse_rows.2 = f32[16,48,768]{2,1,0:T(8,128)} custom-call(f32[2,16,48,768]{3,2,1,0:T(8,128)} %refs_1_.4, f32[2,16,48,768]{3,2,1,0:T(8,128)} %refs_1_.4, bf16[768,768]{1,0:T(8,128)(2,1)S(1)} %get-tuple-element.17.refs_2_.ch_ref.refs_3_, bf16[768,768]{1,0:T(8,128)(2,1)S(1)} %get-tuple-element.18.refs_3_.cl_ref.refs_4_, ...), custom_call_target="tpu_custom_call" | custom-call | flops 10000000000 | bytes 1048576 | tf_op jit(solution)/shard_map/inverse_rows/pallas_call | solution.py:117
  15.0 7.3 %all-to-all-start = ((f32[16,48,768]{2,1,0:T(8,128)}), f32[16,48,768]{2,1,0:T(8,128)}, u32[]{:S(2)}, u32[]{:S(2)}) async-start(f32[16,48,768]{2,1,0:T(8,128)} %inverse_rows.2), calls=%async_computation | async-start | bytes 4718592 | tf_op jit(solution)/shard_map/all_to_all | solution.py:461
  23.6 9.8 %inverse_rows.3 = f32[16,48,768]{2,1,0:T(8,128)} custom-call(f32[2,16,48,768]{3,2,1,0:T(8,128)} %refs_1_.4, f32[2,16,48,768]{3,2,1,0:T(8,128)} %refs_1_.4, bf16[768,768]{1,0:T(8,128)(2,1)S(1)} %get-tuple-element.17.refs_2_.ch_ref.refs_3_, bf16[768,768]{1,0:T(8,128)(2,1)S(1)} %get-tuple-element.18.refs_3_.cl_ref.refs_4_, ...), custom_call_target="tpu_custom_call" | custom-call | flops 10000000000 | bytes 1048576 | tf_op jit(solution)/shard_map/inverse_rows/pallas_call | solution.py:117
  33.4 20.4 %all-to-all-done.in_ref = f32[16,48,768]{2,1,0:T(8,128)} async-done(((f32[16,48,768]{2,1,0:T(8,128)}), f32[16,48,768]{2,1,0:T(8,128)}, u32[]{:S(2)}, u32[]{:S(2)}) %all-to-all-start) | async-done | bytes 2359328 | tf_op jit(solution)/shard_map/all_to_all | solution.py:461
  53.7 4.9 %all-to-all-start.1 = ((f32[16,48,768]{2,1,0:T(8,128)}), f32[16,48,768]{2,1,0:T(8,128)}, u32[]{:S(2)}, u32[]{:S(2)}) async-start(f32[16,48,768]{2,1,0:T(8,128)} %inverse_rows.3), calls=%async_computation.1 | async-start | bytes 4718592 | tf_op jit(solution)/shard_map/all_to_all | solution.py:461
  61.1 6.3 %inverse_columns.2 = (f32[8,48,768]{2,1,0:T(8,128)S(1)}, f32[24,768]{1,0:T(8,128)S(1)}, f32[24,768]{1,0:T(8,128)S(1)}) custom-call(f32[16,48,768]{2,1,0:T(8,128)} %all-to-all-done.in_ref, bf16[768,768]{1,0:T(8,128)(2,1)S(1)} %get-tuple-element.17.refs_2_.ch_ref.refs_3_, bf16[768,768]{1,0:T(8,128)(2,1)S(1)} %get-tuple-element.18.refs_3_.cl_ref.refs_4_, ...), custom_call_target="tpu_custom_call" | custom-call | flops 9600000000 | bytes 1048576 | tf_op jit(solution)/shard_map/inverse_columns/pallas_call | solution.py:162
  67.6 5.6 %collective-permute-start.1 = (f32[3,48,768]{2,1,0:T(8,128)S(1)}, f32[3,48,768]{2,1,0:T(8,128)S(1)}, u32[]{:S(2)}, u32[]{:S(2)}) collective-permute-start(f32[3,48,768]{2,1,0:T(8,128)S(1)} %get-tuple-element.29), channel_id=1, source_target_pairs={{16,0},{32,16},{48,32},{64,48},{80,64},{96,80},{112,96},{0,112},{1... | collective-permute-start | bytes 1327112 | tf_op jit(solution)/shard_map/ppermute | solution.py:178
  73.2 17.5 %collective-permute-done.1.above_ref.refs_4_ = f32[3,48,768]{2,1,0:T(8,128)S(1)} collective-permute-done((f32[3,48,768]{2,1,0:T(8,128)S(1)}, f32[3,48,768]{2,1,0:T(8,128)S(1)}, u32[]{:S(2)}, u32[]{:S(2)}) %collective-permute-start.1) | collective-permute-done | bytes 442400 | tf_op jit(solution)/shard_map/ppermute | solution.py:178
  90.7 5.9 %collective-permute-done.below_ref.refs_1_ = f32[3,48,768]{2,1,0:T(8,128)S(1)} collective-permute-done((f32[3,48,768]{2,1,0:T(8,128)S(1)}, f32[3,48,768]{2,1,0:T(8,128)S(1)}, u32[]{:S(2)}, u32[]{:S(2)}) %collective-permute-start) | collective-permute-done | bytes 442400 | tf_op jit(solution)/shard_map/ppermute | solution.py:178
  106.7 6.3 %inverse_columns.3 = (f32[8,48,768]{2,1,0:T(8,128)S(1)}, f32[24,768]{1,0:T(8,128)S(1)}, f32[24,768]{1,0:T(8,128)S(1)}) custom-call(f32[16,48,768]{2,1,0:T(8,128)} %all-to-all-done.1.in_ref, bf16[768,768]{1,0:T(8,128)(2,1)S(1)} %copy-done.7, bf16[768,768]{1,0:T(8,128)(2,1)S(1)} %copy-done.10, bf16[768,768]{1,0:T(8,128)(2,1)S(1)} %copy-done.14, ...), custom_call_target="tpu_custom_call" | custom-call | flops 9600000000 | bytes 1048576 | tf_op jit(solution)/shard_map/inverse_columns/pallas_call | solution.py:162
  120.3 11.2 %potential.5.x_ref = f32[4,48,768]{2,1,0:T(8,128)} custom-call(s32[3]{0:T(128)} %add_convert_fusion.refs_0_, f32[3,48,768]{2,1,0:T(8,128)} %copy-done.3, f32[8,48,768]{2,1,0:T(8,128)} %copy-done, f32[8,48,768]{2,1,0:T(8,128)} %copy-done.35, f32[3,48,768]{2,1,0:T(8,128)} %copy-done.2, f32[48,768]{1,0:T(8,128)} %copy-done.36, f32[48,768]{1,0:T(8,128)} %copy-done.37, ...), custom_call_target="tpu_custom_call" | custom-call | flops 12000000000 | bytes 1048576 | tf_op jit(solution)/shard_map/potential/pallas_call | solution.py:359
  132.6 5.0 %forward_columns.5 = f32[16,48,384]{2,1,0:T(8,128)} custom-call(f32[4,48,768]{2,1,0:T(8,128)S(1)} %copy-done.33, bf16[768,768]{1,0:T(8,128)(2,1)S(1)} %copy-done.8, bf16[768,768]{1,0:T(8,128)(2,1)S(1)} %copy-done.11, bf16[768,768]{1,0:T(8,128)(2,1)S(1)} %copy-done.15, bf16[768,768]{1,0:T(8,128)(2,1)} %copy-done.20), custom_call_target="tpu_custom_call" | custom-call | flops 4800000000 | bytes 1048576 | tf_op jit(solution)/shard_map/forward_columns/pallas_call | solution.py:395
  137.5 8.1 %all-to-all-start.4 = ((f32[16,48,384]{2,1,0:T(8,128)}), f32[16,48,384]{2,1,0:T(8,128)S(1)}, u32[]{:S(2)}, u32[]{:S(2)}) async-start(f32[16,48,384]{2,1,0:T(8,128)} %forward_columns.5), calls=%async_computation.4 | async-start | bytes 2359296 | tf_op jit(solution)/shard_map/all_to_all | solution.py:461
  145.6 16.3 %potential.4.x_ref = f32[8,48,768]{2,1,0:T(8,128)} custom-call(s32[3]{0:T(128)} %add_convert_fusion.refs_0_, f32[3,48,768]{2,1,0:T(8,128)} %copy-done.3, f32[8,48,768]{2,1,0:T(8,128)} %copy-done, f32[8,48,768]{2,1,0:T(8,128)} %copy-done.35, f32[3,48,768]{2,1,0:T(8,128)} %copy-done.2, f32[48,768]{1,0:T(8,128)} %copy-done.36, f32[48,768]{1,0:T(8,128)} %copy-done.37, ...), custom_call_target="tpu_custom_call" | custom-call | flops 20000000000 | bytes 1048576 | tf_op jit(solution)/shard_map/potential/pallas_call | solution.py:359
  163.3 5.8 %forward_columns.4 = f32[16,48,768]{2,1,0:T(8,128)} custom-call(f32[8,48,768]{2,1,0:T(8,128)S(1)} %copy-done.34, bf16[768,768]{1,0:T(8,128)(2,1)S(1)} %copy-done.8, bf16[768,768]{1,0:T(8,128)(2,1)S(1)} %copy-done.11, bf16[768,768]{1,0:T(8,128)(2,1)S(1)} %copy-done.16, bf16[768,768]{1,0:T(8,128)(2,1)S(1)} %copy-done.24), custom_call_target="tpu_custom_call" | custom-call | flops 9600000000 | bytes 1048576 | tf_op jit(solution)/shard_map/forward_columns/pallas_call | solution.py:395
  169.1 5.7 %all-to-all-start.3 = ((f32[16,48,768]{2,1,0:T(8,128)}), f32[16,48,768]{2,1,0:T(8,128)}, u32[]{:S(2)}, u32[]{:S(2)}) async-start(f32[16,48,768]{2,1,0:T(8,128)} %forward_columns.4), calls=%async_computation.3 | async-start | bytes 4718592 | tf_op jit(solution)/shard_map/all_to_all | solution.py:461
  174.8 11.3 %potential.3.x_ref = f32[4,48,768]{2,1,0:T(8,128)} custom-call(s32[3]{0:T(128)} %add_convert_fusion.refs_0_, f32[3,48,768]{2,1,0:T(8,128)} %copy-done.3, f32[8,48,768]{2,1,0:T(8,128)} %copy-done, f32[8,48,768]{2,1,0:T(8,128)} %copy-done.35, f32[3,48,768]{2,1,0:T(8,128)} %copy-done.2, f32[48,768]{1,0:T(8,128)} %copy-done.36, f32[48,768]{1,0:T(8,128)} %copy-done.37, ...), custom_call_target="tpu_custom_call" | custom-call | flops 12000000000 | bytes 1048576 | tf_op jit(solution)/shard_map/potential/pallas_call | solution.py:359
  187.1 5.0 %forward_columns.3 = f32[16,48,384]{2,1,0:T(8,128)} custom-call(f32[4,48,768]{2,1,0:T(8,128)S(1)} %copy-done.32, bf16[768,768]{1,0:T(8,128)(2,1)S(1)} %copy-done.8, bf16[768,768]{1,0:T(8,128)(2,1)S(1)} %copy-done.11, bf16[768,768]{1,0:T(8,128)(2,1)S(1)} %copy-done.17, bf16[768,768]{1,0:T(8,128)(2,1)} %copy-done.20), custom_call_target="tpu_custom_call" | custom-call | flops 4800000000 | bytes 1048576 | tf_op jit(solution)/shard_map/forward_columns/pallas_call | solution.py:395
  192.1 4.8 %forward_rows.3.refs_2_ = f32[2,16,48,768]{3,2,1,0:T(8,128)} custom-call(s32[3]{0:T(128)S(1)} %copy-done.1, f32[16,48,384]{2,1,0:T(8,128)S(1)} %all-to-all-done.4.refs_1_, bf16[768,768]{1,0:T(8,128)(2,1)S(1)} %copy-done.8, bf16[768,768]{1,0:T(8,128)(2,1)S(1)} %copy-done.11, bf16[768,768]{1,0:T(8,128)(2,1)S(1)} %copy-done.17, bf16[768,768]{1,0:T(8,128)(2,1)S(1)} %copy-done.25), custom_call_target="tpu_custom_call" | custom-call | flops 9200000000 | bytes 1048576 | tf_op jit(solution)/shard_map/forward_rows/pallas_call | solution.py:444
  196.9 9.3 %all-to-all-done.3.refs_1_ = f32[16,48,768]{2,1,0:T(8,128)} async-done(((f32[16,48,768]{2,1,0:T(8,128)}), f32[16,48,768]{2,1,0:T(8,128)}, u32[]{:S(2)}, u32[]{:S(2)}) %all-to-all-start.3) | async-done | bytes 2359328 | tf_op jit(solution)/shard_map/all_to_all | solution.py:461
  206.2 4.9 %all-to-all-start.2 = ((f32[16,48,384]{2,1,0:T(8,128)}), f32[16,48,384]{2,1,0:T(8,128)S(1)}, u32[]{:S(2)}, u32[]{:S(2)}) async-start(f32[16,48,384]{2,1,0:T(8,128)} %forward_columns.3), calls=%async_computation.2 | async-start | bytes 2359296 | tf_op jit(solution)/shard_map/all_to_all | solution.py:461
  213.6 10.5 %forward_rows.4.refs_2_ = f32[2,16,48,768]{3,2,1,0:T(8,128)} custom-call(s32[3]{0:T(128)S(1)} %copy-done.1, f32[16,48,768]{2,1,0:T(8,128)} %all-to-all-done.3.refs_1_, f32[2,16,48,768]{3,2,1,0:T(8,128)} %forward_rows.3.refs_2_, bf16[768,768]{1,0:T(8,128)(2,1)S(1)} %copy-done.8, bf16[768,768]{1,0:T(8,128)(2,1)S(1)} %copy-done.11, ...), custom_call_target="tpu_custom_call", output_to_operand_aliasing={{}: (2, {})} | custom-call | flops 18400000000 | bytes 1048576 | tf_op jit(solution)/shard_map/forward_rows/pallas_call | solution.py:444
  224.1 4.2 %all-to-all-done.2.refs_1_ = f32[16,48,384]{2,1,0:T(8,128)S(1)} async-done(((f32[16,48,384]{2,1,0:T(8,128)}), f32[16,48,384]{2,1,0:T(8,128)S(1)}, u32[]{:S(2)}, u32[]{:S(2)}) %all-to-all-start.2) | async-done | bytes 1179680 | tf_op jit(solution)/shard_map/all_to_all | solution.py:461
  230.9 4.8 %forward_rows.5 = f32[2,16,48,768]{3,2,1,0:T(8,128)} custom-call(s32[3]{0:T(128)S(1)} %copy-done.1, f32[16,48,384]{2,1,0:T(8,128)S(1)} %all-to-all-done.2.refs_1_, f32[2,16,48,768]{3,2,1,0:T(8,128)} %forward_rows.4.refs_2_, bf16[768,768]{1,0:T(8,128)(2,1)S(1)} %copy-done.8, bf16[768,768]{1,0:T(8,128)(2,1)S(1)} %copy-done.11, ...), custom_call_target="tpu_custom_call", output_to_operand_aliasing={{}: (2, {})} | custom-call | flops 9200000000 | bytes 1048576 | tf_op jit(solution)/shard_map/forward_rows/pallas_call | solution.py:444
  (95 shorter events, 33.7 us)
Async XLA Ops:
  3.0 19.4 %copy-start.12 = (bf16[768,768]{1,0:T(8,128)(2,1)}, bf16[768,768]{1,0:T(8,128)(2,1)S(1)}, u32[]{:S(2)}) copy-start(bf16[768,768]{1,0:T(8,128)(2,1)S(1)} %get-tuple-element.19.refs_4_.sh_ref.refs_5_) | copy-start | bytes 3538948
  3.0 55.6 %copy-start.6 = (bf16[768,768]{1,0:T(8,128)(2,1)}, bf16[768,768]{1,0:T(8,128)(2,1)S(1)}, u32[]{:S(2)}) copy-start(bf16[768,768]{1,0:T(8,128)(2,1)S(1)} %get-tuple-element.17.refs_2_.ch_ref.refs_3_) | copy-start | bytes 3538948
  3.0 55.6 %copy-start.9 = (bf16[768,768]{1,0:T(8,128)(2,1)}, bf16[768,768]{1,0:T(8,128)(2,1)S(1)}, u32[]{:S(2)}) copy-start(bf16[768,768]{1,0:T(8,128)(2,1)S(1)} %get-tuple-element.18.refs_3_.cl_ref.refs_4_) | copy-start | bytes 3538948
  15.0 38.7 %all-to-all-start = ((f32[16,48,768]{2,1,0:T(8,128)}), f32[16,48,768]{2,1,0:T(8,128)}, u32[]{:S(2)}, u32[]{:S(2)}) async-start(f32[16,48,768]{2,1,0:T(8,128)} %inverse_rows.2), calls=%async_computation | async-start | bytes 4718592 | tf_op jit(solution)/shard_map/all_to_all | solution.py:461
  53.7 47.9 %all-to-all-start.1 = ((f32[16,48,768]{2,1,0:T(8,128)}), f32[16,48,768]{2,1,0:T(8,128)}, u32[]{:S(2)}, u32[]{:S(2)}) async-start(f32[16,48,768]{2,1,0:T(8,128)} %inverse_rows.3), calls=%async_computation.1 | async-start | bytes 4718592 | tf_op jit(solution)/shard_map/all_to_all | solution.py:461
  67.5 5.7 %copy-start.28 = (f32[24,768]{1,0:T(8,128)}, f32[24,768]{1,0:T(8,128)S(1)}, u32[]{:S(2)}) copy-start(f32[24,768]{1,0:T(8,128)S(1)} %get-tuple-element.23.head_ref) | copy-start | bytes 221188
  67.5 5.7 %copy-start.30 = (f32[24,768]{1,0:T(8,128)}, f32[24,768]{1,0:T(8,128)S(1)}, u32[]{:S(2)}) copy-start(f32[24,768]{1,0:T(8,128)S(1)} %get-tuple-element.24.tail_ref) | copy-start | bytes 221188
  67.5 30.9 %copy-start = (f32[8,48,768]{2,1,0:T(8,128)}, f32[8,48,768]{2,1,0:T(8,128)S(1)}, u32[]{:S(2)}) copy-start(f32[8,48,768]{2,1,0:T(8,128)S(1)} %get-tuple-element.21.refs_2_) | copy-start | bytes 3538948
  67.6 23.1 %collective-permute-start.1 = (f32[3,48,768]{2,1,0:T(8,128)S(1)}, f32[3,48,768]{2,1,0:T(8,128)S(1)}, u32[]{:S(2)}, u32[]{:S(2)}) collective-permute-start(f32[3,48,768]{2,1,0:T(8,128)S(1)} %get-tuple-element.29), channel_id=1, source_target_pairs={{16,0},{32,16},{48,32},{64,48},{80,64},{96,80},{112,96},{0,112},{1... | collective-permute-start | bytes 1327112 | tf_op jit(solution)/shard_map/ppermute | solution.py:178
  73.2 23.4 %collective-permute-start = (f32[3,48,768]{2,1,0:T(8,128)S(1)}, f32[3,48,768]{2,1,0:T(8,128)S(1)}, u32[]{:S(2)}, u32[]{:S(2)}) collective-permute-start(f32[3,48,768]{2,1,0:T(8,128)S(1)} %get-tuple-element.30), channel_id=1, source_target_pairs={{0,16},{16,32},{32,48},{48,64},{64,80},{80,96},{96,112},{112,0},{1... | collective-permute-start | bytes 1327112 | tf_op jit(solution)/shard_map/ppermute | solution.py:178
  90.7 7.8 %copy-start.2 = (f32[3,48,768]{2,1,0:T(8,128)}, f32[3,48,768]{2,1,0:T(8,128)S(1)}, u32[]{:S(2)}) copy-start(f32[3,48,768]{2,1,0:T(8,128)S(1)} %collective-permute-done.1.above_ref.refs_4_) | copy-start | bytes 1327108
  98.5 21.1 %collective-permute-start.2 = (f32[48,768]{1,0:T(8,128)S(1)}, f32[48,768]{1,0:T(8,128)S(1)}, u32[]{:S(2)}, u32[]{:S(2)}) collective-permute-start(f32[48,768]{1,0:T(8,128)S(1)} %get-tuple-element.25), channel_id=1, source_target_pairs={{0,1},{1,2},{2,3},{3,4},{4,5},{5,6},{6,7},{7,8},{8,9},{9,10},{10,1... | collective-permute-start | bytes 442376 | tf_op jit(solution)/shard_map/ppermute | solution.py:178
  101.6 18.0 %collective-permute-start.3 = (f32[48,768]{1,0:T(8,128)S(1)}, f32[48,768]{1,0:T(8,128)S(1)}, u32[]{:S(2)}, u32[]{:S(2)}) collective-permute-start(f32[48,768]{1,0:T(8,128)S(1)} %get-tuple-element.26), channel_id=1, source_target_pairs={{1,0},{2,1},{3,2},{4,3},{5,4},{6,5},{7,6},{8,7},{9,8},{10,9},{11,1... | collective-permute-start | bytes 442376 | tf_op jit(solution)/shard_map/ppermute | solution.py:178
  114.0 3.4 %collective-permute-start.4 = (f32[24,768]{1,0:T(8,128)S(1)}, f32[24,768]{1,0:T(8,128)S(1)}, u32[]{:S(2)}, u32[]{:S(2)}) collective-permute-start(f32[24,768]{1,0:T(8,128)S(1)} %get-tuple-element.27), channel_id=1, source_target_pairs={{0,1},{1,2},{2,3},{3,4},{4,5},{5,6},{6,7},{7,8},{8,9},{9,10},{10,1... | collective-permute-start | bytes 221192 | tf_op jit(solution)/shard_map/ppermute | solution.py:178
  115.8 3.8 %collective-permute-start.5 = (f32[24,768]{1,0:T(8,128)S(1)}, f32[24,768]{1,0:T(8,128)S(1)}, u32[]{:S(2)}, u32[]{:S(2)}) collective-permute-start(f32[24,768]{1,0:T(8,128)S(1)} %get-tuple-element.28), channel_id=1, source_target_pairs={{1,0},{2,1},{3,2},{4,3},{5,4},{6,5},{7,6},{8,7},{9,8},{10,9},{11,1... | collective-permute-start | bytes 221192 | tf_op jit(solution)/shard_map/ppermute | solution.py:178
  120.3 11.2 %copy-start.8 = (bf16[768,768]{1,0:T(8,128)(2,1)S(1)}, bf16[768,768]{1,0:T(8,128)(2,1)}, u32[]{:S(2)}) copy-start(bf16[768,768]{1,0:T(8,128)(2,1)} %copy-done.6) | copy-start | bytes 3538948
  120.3 11.2 %copy-start.11 = (bf16[768,768]{1,0:T(8,128)(2,1)S(1)}, bf16[768,768]{1,0:T(8,128)(2,1)}, u32[]{:S(2)}) copy-start(bf16[768,768]{1,0:T(8,128)(2,1)} %copy-done.9) | copy-start | bytes 3538948
  120.3 11.2 %copy-start.15 = (bf16[768,768]{1,0:T(8,128)(2,1)S(1)}, bf16[768,768]{1,0:T(8,128)(2,1)}, u32[]{:S(2)}) copy-start(bf16[768,768]{1,0:T(8,128)(2,1)} %copy-done.12) | copy-start | bytes 3538948
  137.5 31.6 %all-to-all-start.4 = ((f32[16,48,384]{2,1,0:T(8,128)}), f32[16,48,384]{2,1,0:T(8,128)S(1)}, u32[]{:S(2)}, u32[]{:S(2)}) async-start(f32[16,48,384]{2,1,0:T(8,128)} %forward_columns.5), calls=%async_computation.4 | async-start | bytes 2359296 | tf_op jit(solution)/shard_map/all_to_all | solution.py:461
  145.6 16.3 %copy-start.16 = (bf16[768,768]{1,0:T(8,128)(2,1)S(1)}, bf16[768,768]{1,0:T(8,128)(2,1)}, u32[]{:S(2)}) copy-start(bf16[768,768]{1,0:T(8,128)(2,1)} %copy-done.12) | copy-start | bytes 3538948
  145.6 16.3 %copy-start.24 = (bf16[768,768]{1,0:T(8,128)(2,1)S(1)}, bf16[768,768]{1,0:T(8,128)(2,1)}, u32[]{:S(2)}) copy-start(bf16[768,768]{1,0:T(8,128)(2,1)} %copy-done.20) | copy-start | bytes 3538948
  169.1 37.1 %all-to-all-start.3 = ((f32[16,48,768]{2,1,0:T(8,128)}), f32[16,48,768]{2,1,0:T(8,128)}, u32[]{:S(2)}, u32[]{:S(2)}) async-start(f32[16,48,768]{2,1,0:T(8,128)} %forward_columns.4), calls=%async_computation.3 | async-start | bytes 4718592 | tf_op jit(solution)/shard_map/all_to_all | solution.py:461
  174.8 11.3 %copy-start.17 = (bf16[768,768]{1,0:T(8,128)(2,1)S(1)}, bf16[768,768]{1,0:T(8,128)(2,1)}, u32[]{:S(2)}) copy-start(bf16[768,768]{1,0:T(8,128)(2,1)} %copy-done.12) | copy-start | bytes 3538948
  206.2 22.1 %all-to-all-start.2 = ((f32[16,48,384]{2,1,0:T(8,128)}), f32[16,48,384]{2,1,0:T(8,128)S(1)}, u32[]{:S(2)}, u32[]{:S(2)}) async-start(f32[16,48,384]{2,1,0:T(8,128)} %forward_columns.3), calls=%async_computation.2 | async-start | bytes 2359296 | tf_op jit(solution)/shard_map/all_to_all | solution.py:461
  (27 other events, 39.1 us)
